TPU v7x, 32 devices: a whole 2x2x4 slice. The times are simulated.
32 devices in a mesh: groups: 2 (over x), wide: 16 (over z, y, core).
Axes of the slice: x: 2, y: 2, z: 4, core: 2. Of those that a mesh axis runs over, the one named last changes fastest.
Arguments:
- residual: bfloat16 [4096, 2048], P(('groups', 'wide')), parts along dimension 0, may hold values from -6 to 6
- queries: bfloat16 [4096, 2048], P(('groups', 'wide')), parts along dimension 0, may hold values from -160 to 160
- new_keys: bfloat16 [4096, 256], P(('groups', 'wide')), parts along dimension 0, may hold values from -6 to 6
- new_values: bfloat16 [4096, 256], P(('groups', 'wide')), parts along dimension 0, may hold values from -6 to 6
- cache_keys: bfloat16 [32, 2048, 256], P(('groups', 'wide')), parts along dimension 0, may hold values from -6 to 6
- cache_values: bfloat16 [32, 2048, 256], P(('groups', 'wide')), parts along dimension 0, may hold values from -6 to 6
- cache_len: int32 [32], P('groups'), parts along dimension 0, may hold values from 1 to 2048, 16384 in all
- o_weight: bfloat16 [2048, 2048], P('wide'), may hold values from -0.75 to 0.75
- norm_gain: float32 [2048], replicated, may hold values from 0.5 to 2
- expert_ids: int32 [4096, 8], P(('groups', 'wide')), parts along dimension 0, may hold values from 0 to 15, all different within a row; in each aligned block of 128 rows (0 to 127, 128 to 255, ...) at most 72 rows name the same one
- gate_raw: float32 [4096, 8], P(('groups', 'wide')), parts along dimension 0, may hold values from 0.1 to 1
- w_gate: bfloat16 [16, 2048, 768], P('wide'), may hold values from -0.125 to 0.125
- w_up: bfloat16 [16, 2048, 768], P('wide'), may hold values from -0.125 to 0.125
- w_down: bfloat16 [16, 768, 2048], P('wide'), may hold values from -0.4375 to 0.4375
Outputs:
- layer_out: bfloat16 [4096, 2048], P(('groups', 'wide')), parts along dimension 0
There are 2 independent parts, one for each index of `groups`. A program takes and returns all parts, laid end to end along the dimension named above; an argument that names none is the same for every part. Nothing has to cross between parts.
Inputs may be any that keep to these rules, and one draw needn't show every extreme that they name: `cache_len`: each span's cache holds 1 or more positions; in every part some span has a full cache of 2048 positions and the lengths sum to 16384. `expert_ids`: each token names 8 different experts; among the 128 tokens of one span no expert is named more than 72 times, and in every draw some span names some expert exactly 72 times.
All inputs are finite; a program needn't handle non-finite values.
Results may differ from a plain program's by a relative error of at most 0.01.
Values may be sent and summed in bfloat16 or wider, within the bound.
A program may use at most 128 MiB of HBM per device.

v0:
```python
import functools
import jax
import jax.numpy as jnp
from jax import lax
from jax.experimental import pallas as pl
from jax.experimental.pallas import tpu as pltpu
from jax.sharding import PartitionSpec as P

D = 2048
HEADS = 16
KV_HEADS = 2
HEAD = 128
TOPK = 8
SPAN = 128
PACK = 2
EXP2_SCALE = HEAD ** (-0.5) * 1.4426950408889634


def attention_kernel(length_ref, q_ref, nk_ref, nv_ref, k_ref, v_ref, out_ref):
    tokens = q_ref.shape[0]
    rows = PACK * tokens
    cache = k_ref.shape[1]
    q = jnp.concatenate([q_ref[:, i * HEAD : (i + 1) * HEAD] for i in range(PACK)], axis=0)
    dims = (((1,), (1,)), ((), ()))
    s = lax.dot_general(q, k_ref[0], dims, preferred_element_type=jnp.float32)
    position = lax.broadcasted_iota(jnp.int32, (1, cache), 1)
    s = jnp.where(position < length_ref[0], s, jnp.float32(-1e30))
    s_new = lax.dot_general(q, nk_ref[...], dims, preferred_element_type=jnp.float32)
    row = lax.broadcasted_iota(jnp.int32, (rows, tokens), 0) % tokens
    column = lax.broadcasted_iota(jnp.int32, (rows, tokens), 1)
    s_new = jnp.where(column <= row, s_new, jnp.float32(-1e30))
    top = jnp.maximum(jnp.max(s, axis=1, keepdims=True), jnp.max(s_new, axis=1, keepdims=True))
    w = jnp.exp2((s - top) * EXP2_SCALE)
    w_new = jnp.exp2((s_new - top) * EXP2_SCALE)
    total = jnp.sum(w, axis=1, keepdims=True) + jnp.sum(w_new, axis=1, keepdims=True)
    out = jnp.dot(w.astype(jnp.bfloat16), v_ref[0], preferred_element_type=jnp.float32)
    out += jnp.dot(w_new.astype(jnp.bfloat16), nv_ref[...], preferred_element_type=jnp.float32)
    out = (out / total).astype(out_ref.dtype)
    for i in range(PACK):
        out_ref[:, i * HEAD : (i + 1) * HEAD] = out[i * tokens : (i + 1) * tokens]


def attention(length, queries, new_keys, new_values, cache_keys, cache_values):
    tokens, width = queries.shape
    cache = cache_keys.shape[1]
    per_group = HEADS // KV_HEADS // PACK
    return pl.pallas_call(
        attention_kernel,
        grid=(HEADS // PACK,),
        in_specs=[
            pl.BlockSpec(memory_space=pltpu.SMEM),
            pl.BlockSpec((tokens, PACK * HEAD), lambda i: (0, i)),
            pl.BlockSpec((tokens, HEAD), lambda i: (0, i // per_group)),
            pl.BlockSpec((tokens, HEAD), lambda i: (0, i // per_group)),
            pl.BlockSpec((1, cache, HEAD), lambda i: (0, 0, i // per_group)),
            pl.BlockSpec((1, cache, HEAD), lambda i: (0, 0, i // per_group)),
        ],
        out_specs=pl.BlockSpec((tokens, PACK * HEAD), lambda i: (0, i)),
        out_shape=jax.ShapeDtypeStruct((tokens, width), jnp.bfloat16),
        cost_estimate=pl.CostEstimate(
            flops=4 * tokens * width * (cache + tokens),
            bytes_accessed=4 * cache * KV_HEADS * HEAD + 4 * tokens * width,
            transcendentals=tokens * HEADS * (cache + tokens),
        ),
    )(length, queries, new_keys, new_values, cache_keys, cache_values)


def run_expert(rows_in, gate_w, up_w, down_w):
    gate_part = jnp.dot(rows_in, gate_w, preferred_element_type=jnp.float32)
    up_part = jnp.dot(rows_in, up_w, preferred_element_type=jnp.float32)
    activated = (jax.nn.silu(gate_part) * up_part).astype(jnp.bfloat16)
    return jnp.dot(activated, down_w, preferred_element_type=jnp.float32)


def sparse_experts(normed, expert_ids, shares, gate_w, up_w, down_w, devices):
    token_count = normed.shape[0]
    capacity = SPAN * TOPK // devices + max(2, SPAN * TOPK // (8 * devices))
    flat_ids = expert_ids.reshape(-1)
    one_hot = (flat_ids[:, None] == jnp.arange(devices, dtype=jnp.int32)[None, :]).astype(jnp.int32)
    ranks = jnp.sum(jnp.cumsum(one_hot, axis=0) * one_hot, axis=1) - 1
    slot_index = flat_ids * capacity + ranks
    token_of = jnp.arange(flat_ids.shape[0], dtype=jnp.int32) // TOPK
    slot_token = (
        jnp.full((devices * capacity,), token_count, jnp.int32).at[slot_index].set(token_of)
    )
    padded = jnp.concatenate([normed, jnp.zeros((1, D), jnp.bfloat16)], axis=0)
    outgoing = padded[slot_token].reshape(devices, capacity, D)
    arrived = lax.all_to_all(outgoing, "wide", split_axis=0, concat_axis=0, tiled=True)
    served = run_expert(arrived.reshape(-1, D), gate_w, up_w, down_w).astype(jnp.bfloat16)
    served = served.reshape(devices, capacity, D)
    returned_rows = lax.all_to_all(served, "wide", split_axis=0, concat_axis=0, tiled=True)
    picked = returned_rows.reshape(devices * capacity, D)[slot_index].reshape(token_count, TOPK, D)
    return jnp.sum(picked.astype(jnp.float32) * shares[..., None], axis=1)


LINE = 4
PAIR = 2
EXTRA = 128
DOWN, UP, ACROSS, TWIN = range(4)


def attend(q, key, value, new_key, new_value, length, tokens):
    rows = q.shape[0]
    dims = (((1,), (1,)), ((), ()))
    s = lax.dot_general(q, key, dims, preferred_element_type=jnp.float32)
    position = lax.broadcasted_iota(jnp.int32, (1, key.shape[0]), 1)
    s = jnp.where(position < length, s, jnp.float32(-1e30))
    s_new = lax.dot_general(q, new_key, dims, preferred_element_type=jnp.float32)
    row = lax.broadcasted_iota(jnp.int32, (rows, tokens), 0) % tokens
    column = lax.broadcasted_iota(jnp.int32, (rows, tokens), 1)
    s_new = jnp.where(column <= row, s_new, jnp.float32(-1e30))
    top = jnp.maximum(jnp.max(s, axis=1, keepdims=True), jnp.max(s_new, axis=1, keepdims=True))
    w = jnp.exp2((s - top) * EXP2_SCALE)
    w_new = jnp.exp2((s_new - top) * EXP2_SCALE)
    total = jnp.sum(w, axis=1, keepdims=True) + jnp.sum(w_new, axis=1, keepdims=True)
    out = jnp.dot(w.astype(jnp.bfloat16), value, preferred_element_type=jnp.float32)
    out += jnp.dot(w_new.astype(jnp.bfloat16), new_value, preferred_element_type=jnp.float32)
    return (out / total).astype(jnp.bfloat16)


class Place:
    def __init__(self):
        self.me = lax.axis_index("wide")
        self.core = self.me % 2
        self.y = (self.me // 2) % PAIR
        self.z = self.me // (2 * PAIR)

    def block(self, z, y, core):
        return (z * PAIR + y) * 2 + core

    def towards(self, way):
        z, y, core = self.z, self.y, self.core
        if way == DOWN:
            return self.block(z - 1, y, core)
        if way == UP:
            return self.block(z + 1, y, core)
        if way == ACROSS:
            return self.block(z, 1 - y, core)
        return self.block(z, y, 1 - core)

    def line_at(self, i):
        low = self.z < LINE // 2
        inner = jnp.where(low, self.z, LINE - 1 - self.z)
        near = jnp.where((inner == 0) | (i >= 2), i, 1 - i)
        return jnp.where(low, near, LINE - 1 - near)

    def barrier(self):
        sem = pltpu.get_barrier_semaphore()

        def greet(way):
            pl.semaphore_signal(
                sem,
                inc=1,
                device_id={"wide": self.towards(way)},
                device_id_type=pl.DeviceIdType.MESH,
            )

        pl.when(self.z > 0)(lambda: greet(DOWN))
        pl.when(self.z < LINE - 1)(lambda: greet(UP))
        greet(ACROSS)
        greet(TWIN)
        ends = jnp.where((self.z == 0) | (self.z == LINE - 1), 1, 0)
        pl.semaphore_wait(sem, 4 - ends)


def remote(place, source, target, send_sem, recv_sem, way):
    return pltpu.make_async_remote_copy(
        src_ref=source,
        dst_ref=target,
        send_sem=send_sem,
        recv_sem=recv_sem,
        device_id={"wide": place.towards(way)},
        device_id_type=pl.DeviceIdType.MESH,
    )


class Gather:
    def __init__(self, place, held, send_sem, recv_sem):
        self.place, self.held, self.send_sem, self.recv_sem = place, held, send_sem, recv_sem

    def copy(self, b, way):
        return remote(
            self.place,
            self.held.at[b],
            self.held.at[b],
            self.send_sem.at[b, way],
            self.recv_sem.at[b],
            way,
        )

    def wait(self, b):
        self.copy(b, TWIN).wait_recv()

    def line_ways(self, zb):
        z = self.place.z
        return ((zb >= z) & (z > 0), DOWN), ((zb <= z) & (z < LINE - 1), UP)

    def pass_line(self, zb):
        b = self.place.block(zb, self.place.y, self.place.core)
        for wanted, way in self.line_ways(zb):
            pl.when(wanted)(self.copy(b, way).start)
        self.copy(b, ACROSS).start()
        self.copy(b, TWIN).start()

    def pass_pair(self, zb):
        b = self.place.block(zb, 1 - self.place.y, self.place.core)
        self.wait(b)
        self.copy(b, TWIN).start()

    def drain(self):
        def step(zb, carry):
            b = self.place.block(zb, self.place.y, self.place.core)
            for wanted, way in self.line_ways(zb):
                pl.when(wanted)(self.copy(b, way).wait_send)
            self.copy(b, ACROSS).wait_send()
            self.copy(b, TWIN).wait_send()
            self.copy(self.place.block(zb, 1 - self.place.y, self.place.core), TWIN).wait_send()
            return carry

        lax.fori_loop(0, LINE, step, 0)


def attention_block_kernel(
    length_ref, q_ref, nk_ref, nv_ref, k_ref, v_ref, res_ref, gain_ref, extra_ref, ow_ref,
    mixed_ref, rows_ref, held, attn, own_sem, send_sem, recv_sem,
):
    place = Place()
    tokens = q_ref.shape[0]
    own = pltpu.make_async_copy(ow_ref, held.at[place.me], own_sem)
    own.start()
    place.barrier()
    own.wait()
    gather = Gather(place, held, send_sem, recv_sem)
    gather.pass_line(place.z)
    length = length_ref[place.me]
    per_group = HEADS // KV_HEADS // PACK

    def attend_step(i, carry):
        q = jnp.concatenate(
            [
                q_ref[:, pl.ds(pl.multiple_of((i * PACK + j) * HEAD, HEAD), HEAD)]
                for j in range(PACK)
            ],
            axis=0,
        )
        group = pl.ds(pl.multiple_of(i // per_group * HEAD, HEAD), HEAD)
        out = attend(
            q, k_ref[0, :, group], v_ref[0, :, group], nk_ref[:, group], nv_ref[:, group],
            length, tokens,
        )
        for j in range(PACK):
            attn[:, pl.ds(pl.multiple_of((i * PACK + j) * HEAD, HEAD), HEAD)] = out[
                j * tokens : (j + 1) * tokens
            ]
        return carry

    lax.fori_loop(0, HEADS // PACK, attend_step, 0)
    mixed_ref[...] = res_ref[...].astype(jnp.float32)
    depth = ow_ref.shape[0]

    def project(zb, y):
        gather.wait(place.block(zb, y, 1 - place.core))
        first = place.block(zb, y, 0)
        part = attn[:, pl.ds(pl.multiple_of(first * depth, 2 * depth), 2 * depth)]
        weight = held[pl.ds(first, 2)].reshape(2 * depth, D)
        mixed_ref[...] += jnp.dot(part, weight, preferred_element_type=jnp.float32)

    def step(i, carry):
        @pl.when(i < LINE)
        def _():
            zb = place.line_at(i)

            @pl.when(i > 0)
            def _():
                gather.wait(place.block(zb, place.y, place.core))
                gather.pass_line(zb)

            project(zb, place.y)

        @pl.when(i > 0)
        def _():
            zb = place.line_at(i - 1)
            gather.pass_pair(zb)
            project(zb, 1 - place.y)

        return carry

    lax.fori_loop(0, LINE + 1, step, 0)
    mixed = mixed_ref[...]
    scale = lax.rsqrt(jnp.mean(mixed * mixed, axis=-1, keepdims=True) + 1e-06)
    rows_ref[:, :D] = (mixed * scale * gain_ref[...]).astype(jnp.bfloat16)
    rows_ref[:, D:] = extra_ref[...]
    gather.drain()


def attention_block(
    cache_len, queries, new_keys, new_values, cache_keys, cache_values, residual, gain, extra,
    o_weight, devices,
):
    tokens, width = queries.shape
    cache = cache_keys.shape[1]
    vmem = pl.BlockSpec(memory_space=pltpu.VMEM)
    return pl.pallas_call(
        attention_block_kernel,
        in_specs=[pl.BlockSpec(memory_space=pltpu.SMEM)] + [vmem] * 8
        + [pl.BlockSpec(memory_space=pl.ANY)],
        out_specs=[vmem, vmem],
        out_shape=[
            jax.ShapeDtypeStruct((tokens, D), jnp.float32),
            jax.ShapeDtypeStruct((tokens, D + EXTRA), jnp.bfloat16),
        ],
        scratch_shapes=[
            pltpu.VMEM((devices,) + o_weight.shape, jnp.bfloat16),
            pltpu.VMEM((tokens, width), jnp.bfloat16),
            pltpu.SemaphoreType.DMA,
            pltpu.SemaphoreType.DMA((devices, 4)),
            pltpu.SemaphoreType.DMA((devices,)),
        ],
        compiler_params=pltpu.CompilerParams(collective_id=0, has_side_effects=True),
    )(
        cache_len, queries, new_keys, new_values, cache_keys, cache_values, residual, gain, extra,
        o_weight,
    )


def experts_kernel(
    x_ref, wg_ref, wu_ref, wd_ref, mixed_ref, out_ref,
    rows, part, from_twin, from_pair, from_line, acc, wg, wu, wd,
    own_sem, send_sem, recv_sem, back_send, twin_sem, pair_sem, line_sem,
):
    place = Place()
    me, z, y, core = place.me, place.z, place.y, place.core
    half = x_ref.shape[0] // 2
    devices = rows.shape[0] // 2

    def slot(zb, p, yb, c):
        return ((zb * 2 + p) * PAIR + yb) * 2 + c

    loads = [
        pltpu.make_async_copy(
            x_ref.at[pl.ds(p * half, half)], rows.at[slot(z, p, y, core)], own_sem.at[p]
        )
        for p in range(2)
    ]
    loads += [
        pltpu.make_async_copy(source, target, own_sem.at[2 + k])
        for k, (source, target) in enumerate(((wg_ref, wg), (wu_ref, wu), (wd_ref, wd)))
    ]
    for load in loads:
        load.start()
    place.barrier()
    gather = Gather(place, rows, send_sem, recv_sem)

    def along(b, zb):
        for wanted, way in gather.line_ways(zb):
            pl.when(wanted)(gather.copy(b, way).start)

    def own_out(p):
        loads[p].wait()
        b = slot(z, p, y, core)
        gather.copy(b, ACROSS).start()
        along(b, z)
        gather.copy(b, TWIN).start()

    own_out(1)
    own_out(0)
    lane = lax.broadcasted_iota(jnp.int32, (1, EXTRA), 1)
    chosen = (lane == me) | (lane == me + devices)

    def to_twin(zb, p, yb):
        b = slot(zb, p, yb, 1 - core)
        t = (zb * 2 + p) * PAIR + yb
        return remote(place, part.at[b], from_twin.at[t], back_send.at[b], twin_sem.at[t], TWIN)

    def to_pair(zb, p):
        b = slot(zb, p, 1 - y, core)
        t = LINE if p else zb
        return remote(place, part.at[b], from_pair.at[t], back_send.at[b], pair_sem.at[t], ACROSS)

    def to_line(zb, kind, way):
        b = slot(zb, min(kind, 1), 1 - y if kind == 2 else y, core)
        side = 1 if way == DOWN else 0
        return remote(
            place, part.at[b], from_line.at[side, zb, kind], back_send.at[b],
            line_sem.at[side, zb, kind], way,
        )

    def serve(zb, p):
        gather.wait(slot(zb, p, 0, 1 - core))
        gather.wait(slot(zb, p, 1, 1 - core))
        first = slot(zb, p, 0, 0)
        four = rows[pl.ds(first, 4)].reshape(4 * half, D + EXTRA)
        x = four[:, :D]
        share = jnp.sum(
            jnp.where(chosen, four[:, D:].astype(jnp.float32), 0.0), axis=1, keepdims=True
        )
        gate = jnp.dot(x, wg[...], preferred_element_type=jnp.float32)
        up = jnp.dot(x, wu[...], preferred_element_type=jnp.float32)
        act = (gate / (1.0 + jnp.exp(-gate)) * up).astype(jnp.bfloat16)
        out = jnp.dot(act, wd[...], preferred_element_type=jnp.float32) * share
        part[pl.ds(first, 4)] = out.astype(jnp.bfloat16).reshape(4, half, D)
        to_twin(zb, p, 0).start()
        to_twin(zb, p, 1).start()

    def with_twin(zb, p, yb):
        to_twin(zb, p, yb).wait_recv()
        b = slot(zb, p, yb, core)
        t = (zb * 2 + p) * PAIR + yb
        return part[b].astype(jnp.float32) + from_twin[t].astype(jnp.float32)

    def add_line(zb, kind, way):
        to_line(zb, kind, way).wait_recv()
        side = 1 if way == DOWN else 0
        acc[...] += from_line[side, zb, kind].astype(jnp.float32)

    def fold(zb, kind):
        p = min(kind, 1)
        yb = 1 - y if kind == 2 else y
        acc[...] = with_twin(zb, p, yb)
        if kind == 0:
            to_pair(zb, 0).wait_recv()
            acc[...] += from_pair[zb].astype(jnp.float32)
        pl.when((zb > z) & (z > 0))(lambda: add_line(zb, kind, UP))
        pl.when((zb < z) & (z < LINE - 1))(lambda: add_line(zb, kind, DOWN))
        part[slot(zb, p, yb, core)] = acc[...].astype(jnp.bfloat16)
        pl.when(zb > z)(to_line(zb, kind, UP).start)
        pl.when(zb < z)(to_line(zb, kind, DOWN).start)

    low = z < LINE // 2
    inner = jnp.where(low, z, LINE - 1 - z)

    def fold_at(j):
        near = lax.rem(j + 1 + inner, LINE)
        return jnp.where(low, near, LINE - 1 - near)

    def step(i, carry):
        @pl.when(i < LINE)
        def _():
            zb = place.line_at(i)

            @pl.when(i == 0)
            def _():
                b = slot(z, 1, 1 - y, core)
                gather.wait(b)
                along(b, z)
                gather.copy(b, TWIN).start()
                for load in loads[2:]:
                    load.wait()

            @pl.when(i > 0)
            def _():
                for p, yb in ((1, y), (0, y), (1, 1 - y)):
                    b = slot(zb, p, yb, core)
                    gather.wait(b)
                    if p == 0:
                        gather.copy(b, ACROSS).start()
                    along(b, zb)
                    gather.copy(b, TWIN).start()

            serve(zb, 1)

        @pl.when((i > 0) & (i <= LINE))
        def _():
            zb = place.line_at(i - 1)
            b = slot(zb, 0, 1 - y, core)
            gather.wait(b)
            gather.copy(b, TWIN).start()
            serve(zb, 0)

            part[slot(zb, 0, 1 - y, core)] = with_twin(zb, 0, 1 - y).astype(jnp.bfloat16)
            to_pair(zb, 0).start()

        late = i - 1 - 2 * inner

        @pl.when((late >= 0) & (late < LINE - 1))
        def _():
            zb = fold_at(late)
            fold(zb, 1)
            fold(zb, 2)

        @pl.when((late >= 1) & (late < LINE))
        def _():
            fold(fold_at(late - 1), 0)

        return carry

    lax.fori_loop(0, LINE + 3, step, 0)

    def both_sides(kind):
        pl.when(z > 0)(lambda: add_line(z, kind, UP))
        pl.when(z < LINE - 1)(lambda: add_line(z, kind, DOWN))

    acc[...] = with_twin(z, 1, 1 - y)
    both_sides(2)
    part[slot(z, 1, 1 - y, core)] = acc[...].astype(jnp.bfloat16)
    to_pair(z, 1).start()
    for p in range(2):
        here = pl.ds(p * half, half)
        acc[...] = with_twin(z, p, y) + mixed_ref[here]
        both_sides(p)
        to_pair(z, p).wait_recv()
        acc[...] += from_pair[LINE if p else z].astype(jnp.float32)
        out_ref[here] = acc[...].astype(jnp.bfloat16)
    gather.copy(slot(z, 1, y, core), ACROSS).wait_send()
    to_pair(z, 1).wait_send()

    def settle(zb, carry):
        for p, yb in ((0, y), (1, y), (1, 1 - y)):
            for wanted, way in gather.line_ways(zb):
                pl.when(wanted)(gather.copy(slot(zb, p, yb, core), way).wait_send)
        gather.copy(slot(zb, 0, y, core), ACROSS).wait_send()
        for p in range(2):
            for yb in (y, 1 - y):
                gather.copy(slot(zb, p, yb, core), TWIN).wait_send()
                to_twin(zb, p, yb).wait_send()
        to_pair(zb, 0).wait_send()

        @pl.when(zb != z)
        def _():
            for kind in range(3):
                to_line(zb, kind, UP).wait_send()

        return carry

    lax.fori_loop(0, LINE, settle, 0)


def experts_block(x, gate_w, up_w, down_w, mixed, devices):
    tokens = x.shape[0]
    half = tokens // 2
    vmem = pl.BlockSpec(memory_space=pltpu.VMEM)
    whole = pl.BlockSpec(memory_space=pl.ANY)

    def held(*lead):
        return pltpu.VMEM(lead + (half, D), jnp.bfloat16)

    dma = pltpu.SemaphoreType.DMA
    return pl.pallas_call(
        experts_kernel,
        in_specs=[whole] * 4 + [vmem],
        out_specs=vmem,
        out_shape=jax.ShapeDtypeStruct((tokens, D), jnp.bfloat16),
        scratch_shapes=[
            pltpu.VMEM((2 * devices, half, x.shape[1]), jnp.bfloat16),
            held(2 * devices),
            held(devices),
            held(LINE + 1),
            held(2, LINE, 3),
            pltpu.VMEM((half, D), jnp.float32),
            pltpu.VMEM(gate_w.shape, jnp.bfloat16),
            pltpu.VMEM(up_w.shape, jnp.bfloat16),
            pltpu.VMEM(down_w.shape, jnp.bfloat16),
            dma((5,)),
            dma((2 * devices, 4)),
            dma((2 * devices,)),
            dma((2 * devices,)),
            dma((devices,)),
            dma((LINE + 1,)),
            dma((2, LINE, 3)),
        ],
        compiler_params=pltpu.CompilerParams(collective_id=1, has_side_effects=True),
    )(x, gate_w, up_w, down_w, mixed)


def grid_device(
    residual, queries, new_keys, new_values, cache_keys, cache_values, cache_len, o_weight,
    norm_gain, expert_ids, gate_raw, w_gate, w_up, w_down,
):
    devices = lax.axis_size("wide")
    shares = gate_raw / jnp.sum(gate_raw, axis=-1, keepdims=True)
    hits = expert_ids[:, :, None] == jnp.arange(devices, dtype=jnp.int32)[None, None, :]
    share_of = jnp.sum(jnp.where(hits, shares[..., None], 0.0), axis=1)
    coarse = share_of.astype(jnp.bfloat16)
    fine = (share_of - coarse.astype(jnp.float32)).astype(jnp.bfloat16)
    extra = jnp.pad(jnp.concatenate([coarse, fine], axis=1), ((0, 0), (0, EXTRA - 2 * devices)))
    mixed, rows = attention_block(
        cache_len, queries, new_keys, new_values, cache_keys, cache_values, residual,
        norm_gain.reshape(1, D), extra, o_weight, devices,
    )
    return experts_block(rows, w_gate[0], w_up[0], w_down[0], mixed, devices)


def per_device(
    residual,
    queries,
    new_keys,
    new_values,
    cache_keys,
    cache_values,
    cache_len,
    o_weight,
    norm_gain,
    expert_ids,
    gate_raw,
    w_gate,
    w_up,
    w_down,
):
    devices = lax.axis_size("wide")
    me = lax.axis_index("wide")
    length = lax.dynamic_slice_in_dim(cache_len, me, 1, 0)
    attn = attention(length, queries, new_keys, new_values, cache_keys, cache_values)
    projected = jnp.dot(
        attn,
        lax.all_gather(o_weight, "wide", axis=0, tiled=True),
        preferred_element_type=jnp.float32,
    )
    mixed = residual.astype(jnp.float32) + projected
    normed = (
        mixed * lax.rsqrt(jnp.mean(mixed * mixed, axis=-1, keepdims=True) + 1e-06) * norm_gain
    ).astype(jnp.bfloat16)
    shares = gate_raw / jnp.sum(gate_raw, axis=-1, keepdims=True)
    routed = sparse_experts(normed, expert_ids, shares, w_gate[0], w_up[0], w_down[0], devices)
    return (mixed + routed).astype(jnp.bfloat16)


def solution(mesh):
    rows = P(("groups", "wide"), None)
    blocks = P(("groups", "wide"), None, None)
    weights = P("wide", None, None)
    placed = (rows, rows, rows, rows, blocks, blocks, P("groups"), P("wide", None), P())
    placed += (rows, rows, weights, weights, weights)
    grid = mesh.shape["wide"] == LINE * PAIR * 2
    return jax.shard_map(
        grid_device if grid else per_device,
        mesh=mesh,
        in_specs=placed,
        out_specs=rows,
        check_vma=False,
    )
```

profile of v0, /device:TPU:0, one launch (start us, length us, event | category | flops | bytes accessed | tf_op | source)
XLA Modules:
  0.0 191.5 jit_solution(12481138170109267515)
XLA Ops:
  0.0 0.7 reduce_sum.18
  0.7 0.7 broadcast_divide_fusion
  1.4 0.7 select_reduce_fusion
  2.1 0.1 copy.20
  2.2 0.6 pad.4.extra_ref
  2.9 62.1 %shard_map.136 = (f32[128,2048]{1,0:T(8,128)}, bf16[128,2176]{1,0:T(8,128)(2,1)}) custom-call(s32[16]{0:T(128)} %length_ref.1, bf16[128,2048]{1,0:T(8,128)(2,1)} %q_ref.1, bf16[128,256]{1,0:T(8,128)(2,1)} %nk_ref.1, bf16[128,256]{1,0:T(8,128)(2,1)} %nv_ref.1, bf16[1,2048,256]{2,1,0:T(8,128)(2,1)} %k_ref.1, bf16[1,2048,256]{2,1,0:T(8,128)(2,1)} %v_ref.1, ...), custom_call_target="tpu_custom_call" | custom-call | tf_op jit(solution)/shard_map/pallas_call | solution.py:303
  65.0 124.6 %shard_map.137 = bf16[128,2048]{1,0:T(8,128)(2,1)} custom-call(bf16[128,2176]{1,0:T(8,128)(2,1)} %get-tuple-element.7.x_ref, bf16[2048,768]{1,0:T(8,128)(2,1)} %bitcast.4, bf16[2048,768]{1,0:T(8,128)(2,1)} %bitcast.5, bf16[768,2048]{1,0:T(8,128)(2,1)} %bitcast.6, f32[128,2048]{1,0:T(8,128)} %get-tuple-element.8.mixed_ref), custom_call_target="tpu_custom_call" | custom-call | tf_op jit(solution)/shard_map/pallas_call | solution.py:538
  189.6 1.9 copy.22
  (2 shorter events, 0.0 us)
where the time goes:
time: 192 us
  Pallas kernels  187 us (97%)
  local copies, waits for them, and re-layouts  2.63 us (1%)
  other arithmetic  2.11 us (1%)
    pallas_call x1, Pallas kernels, experts_block(): pl.pallas_call(experts_kernel, in_specs=[whole] * 4 + [vmem], out_specs=v...  125 us
    pallas_call x1, Pallas kernels, attention_block(): pl.pallas_call(attention_block_kernel, in_specs=[pl.BlockSpec(memory_spac...  62.1 us

commit v1 on v0

--- a/solution.py
+++ b/solution.py
@@ -76,8 +76,13 @@
     token_count = normed.shape[0]
     capacity = SPAN * TOPK // devices + max(2, SPAN * TOPK // (8 * devices))
     flat_ids = expert_ids.reshape(-1)
-    one_hot = (flat_ids[:, None] == jnp.arange(devices, dtype=jnp.int32)[None, :]).astype(jnp.int32)
-    ranks = jnp.sum(jnp.cumsum(one_hot, axis=0) * one_hot, axis=1) - 1
+    named = expert_ids[:, :, None] == jnp.arange(devices, dtype=jnp.int32)[None, None, :]
+    earlier = jnp.tril(jnp.ones((token_count, token_count), jnp.bfloat16), -1)
+    before = jnp.dot(
+        earlier, jnp.any(named, axis=1).astype(jnp.bfloat16), preferred_element_type=jnp.float32
+    )
+    ranks = jnp.sum(jnp.where(named, before[:, None, :], 0.0), axis=-1)
+    ranks = ranks.astype(jnp.int32).reshape(-1)
     slot_index = flat_ids * capacity + ranks
     token_of = jnp.arange(flat_ids.shape[0], dtype=jnp.int32) // TOPK
     slot_token = (
@@ -144,7 +149,7 @@
         near = jnp.where((inner == 0) | (i >= 2), i, 1 - i)
         return jnp.where(low, near, LINE - 1 - near)
 
-    def barrier(self):
+    def barrier(self, with_x=False):
         sem = pltpu.get_barrier_semaphore()
 
         def greet(way):
@@ -159,65 +164,60 @@
         pl.when(self.z < LINE - 1)(lambda: greet(UP))
         greet(ACROSS)
         greet(TWIN)
+        if with_x:
+            pl.semaphore_signal(
+                sem, inc=1, device_id={"groups": 1 - lax.axis_index("groups")},
+                device_id_type=pl.DeviceIdType.MESH,
+            )
         ends = jnp.where((self.z == 0) | (self.z == LINE - 1), 1, 0)
-        pl.semaphore_wait(sem, 4 - ends)
-
-
-def remote(place, source, target, send_sem, recv_sem, way):
-    return pltpu.make_async_remote_copy(
-        src_ref=source,
-        dst_ref=target,
-        send_sem=send_sem,
-        recv_sem=recv_sem,
-        device_id={"wide": place.towards(way)},
-        device_id_type=pl.DeviceIdType.MESH,
-    )
-
-
-class Gather:
-    def __init__(self, place, held, send_sem, recv_sem):
-        self.place, self.held, self.send_sem, self.recv_sem = place, held, send_sem, recv_sem
-
-    def copy(self, b, way):
-        return remote(
-            self.place,
-            self.held.at[b],
-            self.held.at[b],
-            self.send_sem.at[b, way],
-            self.recv_sem.at[b],
-            way,
-        )
-
-    def wait(self, b):
-        self.copy(b, TWIN).wait_recv()
-
-    def line_ways(self, zb):
-        z = self.place.z
-        return ((zb >= z) & (z > 0), DOWN), ((zb <= z) & (z < LINE - 1), UP)
-
-    def pass_line(self, zb):
-        b = self.place.block(zb, self.place.y, self.place.core)
-        for wanted, way in self.line_ways(zb):
-            pl.when(wanted)(self.copy(b, way).start)
-        self.copy(b, ACROSS).start()
-        self.copy(b, TWIN).start()
-
-    def pass_pair(self, zb):
-        b = self.place.block(zb, 1 - self.place.y, self.place.core)
-        self.wait(b)
-        self.copy(b, TWIN).start()
-
-    def drain(self):
-        def step(zb, carry):
-            b = self.place.block(zb, self.place.y, self.place.core)
-            for wanted, way in self.line_ways(zb):
-                pl.when(wanted)(self.copy(b, way).wait_send)
-            self.copy(b, ACROSS).wait_send()
-            self.copy(b, TWIN).wait_send()
-            self.copy(self.place.block(zb, 1 - self.place.y, self.place.core), TWIN).wait_send()
-            return carry
-
-        lax.fori_loop(0, LINE, step, 0)
+        pl.semaphore_wait(sem, (5 if with_x else 4) - ends)
+
+
+UPN, DOWNN = 0, 1
+XWAY = 4
+TILE = 16
+P0, P1, PR, Q0, Q1, QS = range(6)
+A_SLOTS = 6
+
+
+def gather_events(*items):
+    codes = [kind * 4 + nb for kind, nb in items]
+    codes += [31] * (A_SLOTS - len(codes))
+    return sum(c << (5 * j) for j, c in enumerate(codes))
+
+
+A_END = (
+    gather_events(), gather_events(), gather_events(),
+    gather_events((Q0, 0), (P0, 1)),
+    gather_events((Q1, 0)),
+    gather_events((P1, 1)),
+    gather_events((QS, 0), (Q0, 1)),
+    gather_events((P0, 2), (PR, 1), (Q1, 1)),
+    gather_events((P1, 2), (QS, 1)),
+    gather_events((Q0, 2), (PR, 2), (P0, 3)),
+    gather_events((Q1, 2), (QS, 2)),
+    gather_events((P1, 3), (Q0, 3), (PR, 3), (Q1, 3), (QS, 3)),
+)
+A_INNER = (
+    gather_events(), gather_events(), gather_events(),
+    gather_events((Q0, 1), (P0, 0), (P0, 2)),
+    gather_events((Q1, 1)),
+    gather_events((P1, 0), (P1, 2)),
+    gather_events((QS, 1), (Q0, 0)),
+    gather_events((P0, 3), (PR, 0), (PR, 2)),
+    gather_events((Q0, 2), (P1, 3)),
+    gather_events((Q1, 0), (QS, 0)),
+    gather_events((Q1, 2), (QS, 2)),
+    gather_events((Q0, 3), (PR, 3), (Q1, 3), (QS, 3)),
+)
+
+
+def pick(index, inner, ends, inners):
+    at_end, at_inner = jnp.int32(ends[0]), jnp.int32(inners[0])
+    for k in range(1, len(ends)):
+        at_end = jnp.where(index == k, jnp.int32(ends[k]), at_end)
+        at_inner = jnp.where(index == k, jnp.int32(inners[k]), at_inner)
+    return jnp.where(inner == 1, at_inner, at_end)
 
 
 def attention_block_kernel(
@@ -225,17 +225,124 @@
     mixed_ref, rows_ref, held, attn, own_sem, send_sem, recv_sem,
 ):
     place = Place()
+    z, y, core = place.z, place.y, place.core
+    group = lax.axis_index("groups")
     tokens = q_ref.shape[0]
+    depth = ow_ref.shape[0]
+    low = z < LINE // 2
+    inner = jnp.where(low, z, LINE - 1 - z)
+    step_up = jnp.where(low, 1, -1)
     own = pltpu.make_async_copy(ow_ref, held.at[place.me], own_sem)
     own.start()
-    place.barrier()
+    place.barrier(True)
     own.wait()
-    gather = Gather(place, held, send_sem, recv_sem)
-    gather.pass_line(place.z)
+
+    third = depth // 8 * 2
+    half = depth // 8 * 3
+    last = depth - half
+    span = {
+        P0: (jnp.where(group == 0, 0, last), half),
+        P1: (jnp.where(group == 0, half, third), half),
+        PR: (jnp.where(group == 0, depth - third, 0), third),
+        Q0: (jnp.where(group == 0, 0, last), half),
+        Q1: (half, depth - 2 * half),
+        QS: (jnp.where(group == 0, last, 0), half),
+    }
+    given = {PR: (jnp.where(group == 0, 0, depth - third), third), QS: span[Q0]}
+
+    def real(nb):
+        return jnp.where(low, nb, LINE - 1 - nb)
+
+    def device(way):
+        if way == XWAY:
+            return {"groups": 1 - group}
+        if way == UPN:
+            return {"wide": place.block(z + step_up, y, core)}
+        if way == DOWNN:
+            return {"wide": place.block(z - step_up, y, core)}
+        return {"wide": place.towards(way)}
+
+    def copy(b, what, way):
+        start, size = given[what] if way == XWAY else span[what]
+        if not isinstance(start, int):
+            start = pl.multiple_of(start, TILE)
+        ref = held.at[b, pl.ds(start, size)]
+        i = what % 3
+        return pltpu.make_async_remote_copy(
+            src_ref=ref, dst_ref=ref, send_sem=send_sem.at[b, i, way], recv_sem=recv_sem.at[b, i],
+            device_id=device(way), device_id_type=pl.DeviceIdType.MESH,
+        )
+
+    def whole(b):
+        return pltpu.make_async_remote_copy(
+            src_ref=held.at[b], dst_ref=held.at[b], send_sem=send_sem.at[b, 2, TWIN],
+            recv_sem=recv_sem.at[b, 0], device_id=device(TWIN),
+            device_id_type=pl.DeviceIdType.MESH,
+        )
+
+    def block_at(nb, yb, c):
+        return place.block(real(nb), yb, c)
+
+    me = place.me
+    copy(me, P0, UPN).start()
+    pl.when(inner == 1)(copy(me, P0, DOWNN).start)
+    copy(me, Q0, ACROSS).start()
+    copy(me, P1, UPN).start()
+    pl.when(inner == 1)(copy(me, P1, DOWNN).start)
+    copy(me, Q1, ACROSS).start()
+    whole(me).start()
+
+    def happen(code):
+        nb = lax.rem(code, 4)
+        kind = code // 4
+        own_b = block_at(nb, y, core)
+        other_b = block_at(nb, 1 - y, core)
+
+        def line(what):
+            pl.when(nb < inner)(copy(own_b, what, UPN).start)
+            pl.when((nb > inner) & (inner == 1))(copy(own_b, what, DOWNN).start)
+
+        @pl.when(kind == P0)
+        def _():
+            copy(own_b, P0, TWIN).wait_recv()
+            line(P0)
+            copy(own_b, Q0, ACROSS).start()
+            copy(own_b, PR, XWAY).start()
+            copy(own_b, P0, TWIN).start()
+
+        @pl.when(kind == P1)
+        def _():
+            copy(own_b, P1, TWIN).wait_recv()
+            line(P1)
+            copy(own_b, Q1, ACROSS).start()
+            copy(own_b, P1, TWIN).start()
+
+        @pl.when(kind == PR)
+        def _():
+            copy(own_b, PR, TWIN).wait_recv()
+            copy(own_b, PR, TWIN).start()
+
+        @pl.when(kind == Q0)
+        def _():
+            copy(other_b, Q0, TWIN).wait_recv()
+            copy(other_b, QS, XWAY).start()
+            copy(other_b, Q0, TWIN).start()
+
+        @pl.when(kind == Q1)
+        def _():
+            copy(other_b, Q1, TWIN).wait_recv()
+            copy(other_b, Q1, TWIN).start()
+
+        @pl.when(kind == QS)
+        def _():
+            copy(other_b, QS, TWIN).wait_recv()
+            copy(other_b, QS, TWIN).start()
+
     length = length_ref[place.me]
+    attends = HEADS // PACK
     per_group = HEADS // KV_HEADS // PACK
 
-    def attend_step(i, carry):
+    def attend_step(i):
         q = jnp.concatenate(
             [
                 q_ref[:, pl.ds(pl.multiple_of((i * PACK + j) * HEAD, HEAD), HEAD)]
@@ -243,54 +350,93 @@
             ],
             axis=0,
         )
-        group = pl.ds(pl.multiple_of(i // per_group * HEAD, HEAD), HEAD)
+        columns = pl.ds(pl.multiple_of(i // per_group * HEAD, HEAD), HEAD)
         out = attend(
-            q, k_ref[0, :, group], v_ref[0, :, group], nk_ref[:, group], nv_ref[:, group],
-            length, tokens,
+            q, k_ref[0, :, columns], v_ref[0, :, columns], nk_ref[:, columns],
+            nv_ref[:, columns], length, tokens,
         )
         for j in range(PACK):
             attn[:, pl.ds(pl.multiple_of((i * PACK + j) * HEAD, HEAD), HEAD)] = out[
                 j * tokens : (j + 1) * tokens
             ]
-        return carry
-
-    lax.fori_loop(0, HEADS // PACK, attend_step, 0)
+
     mixed_ref[...] = res_ref[...].astype(jnp.float32)
-    depth = ow_ref.shape[0]
-
-    def project(zb, y):
-        gather.wait(place.block(zb, y, 1 - place.core))
-        first = place.block(zb, y, 0)
+
+    def project(nb, is_own):
+        yb = jnp.where(is_own, y, 1 - y)
+        b = block_at(nb, yb, 1 - core)
+
+        @pl.when(is_own & (nb == inner))
+        def _():
+            whole(b).wait_recv()
+
+        @pl.when(is_own & (nb != inner))
+        def _():
+            for what in (P0, P1, PR):
+                copy(b, what, TWIN).wait_recv()
+
+        @pl.when(jnp.logical_not(is_own))
+        def _():
+            for what in (Q0, Q1, QS):
+                copy(b, what, TWIN).wait_recv()
+
+        first = block_at(nb, yb, 0)
         part = attn[:, pl.ds(pl.multiple_of(first * depth, 2 * depth), 2 * depth)]
         weight = held[pl.ds(first, 2)].reshape(2 * depth, D)
         mixed_ref[...] += jnp.dot(part, weight, preferred_element_type=jnp.float32)
 
-    def step(i, carry):
-        @pl.when(i < LINE)
-        def _():
-            zb = place.line_at(i)
-
-            @pl.when(i > 0)
-            def _():
-                gather.wait(place.block(zb, place.y, place.core))
-                gather.pass_line(zb)
-
-            project(zb, place.y)
-
-        @pl.when(i > 0)
-        def _():
-            zb = place.line_at(i - 1)
-            gather.pass_pair(zb)
-            project(zb, 1 - place.y)
+    def step(s, carry):
+        def one(j, word):
+            code = lax.rem(word, 32)
+            pl.when(code < 31)(lambda: happen(code))
+            return word // 32
+
+        lax.fori_loop(0, A_SLOTS, one, pick(s, inner, A_END, A_INNER))
+        pl.when(s < attends)(lambda: attend_step(s))
+
+        @pl.when(s >= attends)
+        def _():
+            nb = pick(s - attends, inner, (0, 1, 2, 3), (1, 0, 2, 3))
+
+            def both(k, inside):
+                project(nb, k == 0)
+                return inside
+
+            lax.fori_loop(0, 2, both, 0)
 
         return carry
 
-    lax.fori_loop(0, LINE + 1, step, 0)
+    lax.fori_loop(0, len(A_END), step, 0)
     mixed = mixed_ref[...]
     scale = lax.rsqrt(jnp.mean(mixed * mixed, axis=-1, keepdims=True) + 1e-06)
     rows_ref[:, :D] = (mixed * scale * gain_ref[...]).astype(jnp.bfloat16)
     rows_ref[:, D:] = extra_ref[...]
-    gather.drain()
+
+    def settle(nb, carry):
+        own_b = block_at(nb, y, core)
+        other_b = block_at(nb, 1 - y, core)
+        for what in (P0, P1):
+            pl.when(nb <= inner)(copy(own_b, what, UPN).wait_send)
+            pl.when((nb >= inner) & (inner == 1))(copy(own_b, what, DOWNN).wait_send)
+        copy(own_b, Q0, ACROSS).wait_send()
+        copy(own_b, Q1, ACROSS).wait_send()
+
+        @pl.when(nb == inner)
+        def _():
+            whole(own_b).wait_send()
+
+        @pl.when(nb != inner)
+        def _():
+            copy(own_b, PR, XWAY).wait_send()
+            for what in (P0, P1, PR):
+                copy(own_b, what, TWIN).wait_send()
+
+        copy(other_b, QS, XWAY).wait_send()
+        for what in (Q0, Q1, QS):
+            copy(other_b, what, TWIN).wait_send()
+        return carry
+
+    lax.fori_loop(0, LINE, settle, 0)
 
 
 def attention_block(
@@ -313,14 +459,67 @@
             pltpu.VMEM((devices,) + o_weight.shape, jnp.bfloat16),
             pltpu.VMEM((tokens, width), jnp.bfloat16),
             pltpu.SemaphoreType.DMA,
-            pltpu.SemaphoreType.DMA((devices, 4)),
-            pltpu.SemaphoreType.DMA((devices,)),
+            pltpu.SemaphoreType.DMA((devices, 3, 5)),
+            pltpu.SemaphoreType.DMA((devices, 3)),
         ],
-        compiler_params=pltpu.CompilerParams(collective_id=0, has_side_effects=True),
+        compiler_params=pltpu.CompilerParams(
+            collective_id=0, has_side_effects=True, vmem_limit_bytes=60 << 20
+        ),
     )(
         cache_len, queries, new_keys, new_values, cache_keys, cache_values, residual, gain, extra,
         o_weight,
     )
+
+
+SUBS = 2
+PA, PB, PC, PD = range(4)
+ARRIVE, OWN_UP, OWN_DOWN, NOTHING = range(4)
+WORDS = 3
+
+
+def event(kind, nb, piece, h):
+    return ((kind * 4 + nb) * 4 + piece) * 2 + h
+
+
+def events(text):
+    kinds = {"u": OWN_UP, "d": OWN_DOWN}
+    codes = []
+    for item in (text[k : k + 3] for k in range(0, len(text), 3)):
+        if item[0] in kinds:
+            codes.append(event(kinds[item[0]], 0, "abcd".index(item[1]), int(item[2])))
+        else:
+            codes.append(event(ARRIVE, int(item[0]), "abcd".index(item[1]), int(item[2])))
+    assert len(codes) <= 4 * WORDS
+    codes += [127] * (4 * WORDS - len(codes))
+    return [sum(c << (7 * j) for j, c in enumerate(codes[4 * w : 4 * w + 4])) for w in range(WORDS)]
+
+
+def folds(text):
+    codes = [int(item[0]) * 4 + int(item[1]) for item in (text[k : k + 2] for k in range(0, len(text), 2))]
+    codes += [15] * (7 - len(codes))
+    return sum(c << (4 * j) for j, c in enumerate(codes))
+
+
+END_STEPS = (
+    ("0b0ub00b1ub1uc0uc11a0", "01", ""),
+    ("0d00d12a0", "00", ""),
+    ("3a03a13b03b1", "31", "3132"),
+    ("3c03c13d03d1", "30", ""),
+    ("2a12b02b1", "21", "302122"),
+    ("2c02c12d02d1", "20", ""),
+    ("1a11b01b1", "11", "201112"),
+    ("1c01c11d01d1", "10", "10"),
+)
+INNER_STEPS = (
+    ("0a02a01b00a13a01b1", "11", ""),
+    ("0b03a11d00b13b01d1", "10", ""),
+    ("0c03b10c13c0ua1ub0ub1uc0uc1", "01", ""),
+    ("3c10d00d1", "00", ""),
+    ("2a1da1db0", "31", ""),
+    ("2b03d03d12b1db1", "30", ""),
+    ("2c02c1dc0dc1", "21", "3132"),
+    ("2d02d1", "20", "30010221002220"),
+)
 
 
 def experts_kernel(
@@ -331,65 +530,103 @@
     place = Place()
     me, z, y, core = place.me, place.z, place.y, place.core
     half = x_ref.shape[0] // 2
-    devices = rows.shape[0] // 2
+    sub = half // SUBS
+    devices = rows.shape[0] // (2 * SUBS)
+    low = z < LINE // 2
+    inner = jnp.where(low, z, LINE - 1 - z)
+    step_up = jnp.where(low, 1, -1)
+    side_up = jnp.where(low, 0, 1)
+
+    def real(nb):
+        return jnp.where(low, nb, LINE - 1 - nb)
+
+    def target(way):
+        if way == UPN:
+            return place.block(z + step_up, y, core)
+        if way == DOWNN:
+            return place.block(z - step_up, y, core)
+        return place.towards(way)
+
+    def send(source, dest, send_one, recv_one, way):
+        return pltpu.make_async_remote_copy(
+            src_ref=source, dst_ref=dest, send_sem=send_one, recv_sem=recv_one,
+            device_id={"wide": target(way)}, device_id_type=pl.DeviceIdType.MESH,
+        )
 
     def slot(zb, p, yb, c):
         return ((zb * 2 + p) * PAIR + yb) * 2 + c
 
+    def copy(b, h, way):
+        t = b * SUBS + h
+        return send(rows.at[t], rows.at[t], send_sem.at[t, way], recv_sem.at[t], way)
+
     loads = [
         pltpu.make_async_copy(
-            x_ref.at[pl.ds(p * half, half)], rows.at[slot(z, p, y, core)], own_sem.at[p]
+            x_ref.at[pl.ds(p * half + h * sub, sub)],
+            rows.at[slot(z, p, y, core) * SUBS + h],
+            own_sem.at[p * SUBS + h],
         )
         for p in range(2)
+        for h in range(SUBS)
     ]
     loads += [
-        pltpu.make_async_copy(source, target, own_sem.at[2 + k])
-        for k, (source, target) in enumerate(((wg_ref, wg), (wu_ref, wu), (wd_ref, wd)))
+        pltpu.make_async_copy(source, dest, own_sem.at[2 * SUBS + k])
+        for k, (source, dest) in enumerate(((wg_ref, wg), (wu_ref, wu), (wd_ref, wd)))
     ]
     for load in loads:
         load.start()
     place.barrier()
-    gather = Gather(place, rows, send_sem, recv_sem)
-
-    def along(b, zb):
-        for wanted, way in gather.line_ways(zb):
-            pl.when(wanted)(gather.copy(b, way).start)
-
-    def own_out(p):
-        loads[p].wait()
-        b = slot(z, p, y, core)
-        gather.copy(b, ACROSS).start()
-        along(b, z)
-        gather.copy(b, TWIN).start()
-
-    own_out(1)
-    own_out(0)
+    own_a = slot(z, 1, y, core)
+    own_c = slot(z, 0, y, core)
+    for h in range(SUBS):
+        loads[SUBS + h].wait()
+        copy(own_a, h, ACROSS).start()
+        if h == 0:
+            copy(own_a, h, UPN).start()
+            pl.when(inner == 1)(copy(own_a, h, DOWNN).start)
+        else:
+            pl.when(inner == 0)(copy(own_a, h, UPN).start)
+        copy(own_a, h, TWIN).start()
+    for h in range(SUBS):
+        loads[h].wait()
+        copy(own_c, h, ACROSS).start()
+        copy(own_c, h, TWIN).start()
+
     lane = lax.broadcasted_iota(jnp.int32, (1, EXTRA), 1)
     chosen = (lane == me) | (lane == me + devices)
 
     def to_twin(zb, p, yb):
         b = slot(zb, p, yb, 1 - core)
         t = (zb * 2 + p) * PAIR + yb
-        return remote(place, part.at[b], from_twin.at[t], back_send.at[b], twin_sem.at[t], TWIN)
+        return send(part.at[b], from_twin.at[t], back_send.at[b], twin_sem.at[t], TWIN)
 
     def to_pair(zb, p):
         b = slot(zb, p, 1 - y, core)
         t = LINE if p else zb
-        return remote(place, part.at[b], from_pair.at[t], back_send.at[b], pair_sem.at[t], ACROSS)
+        return send(part.at[b], from_pair.at[t], back_send.at[b], pair_sem.at[t], ACROSS)
+
+    def kind_slot(zb, kind):
+        p = jnp.minimum(kind, 1)
+        yb = jnp.where(kind == 2, 1 - y, y)
+        return p, yb, slot(zb, p, yb, core)
 
     def to_line(zb, kind, way):
-        b = slot(zb, min(kind, 1), 1 - y if kind == 2 else y, core)
-        side = 1 if way == DOWN else 0
-        return remote(
-            place, part.at[b], from_line.at[side, zb, kind], back_send.at[b],
+        b = kind_slot(zb, kind)[2]
+        side = side_up if way == UPN else 1 - side_up
+        return send(
+            part.at[b], from_line.at[side, zb, kind], back_send.at[b],
             line_sem.at[side, zb, kind], way,
         )
 
+    def wait_rows(b):
+        for h in range(SUBS):
+            copy(b, h, TWIN).wait_recv()
+
     def serve(zb, p):
-        gather.wait(slot(zb, p, 0, 1 - core))
-        gather.wait(slot(zb, p, 1, 1 - core))
+        wait_rows(slot(zb, p, 0, 1 - core))
+        wait_rows(slot(zb, p, 1, 1 - core))
         first = slot(zb, p, 0, 0)
-        four = rows[pl.ds(first, 4)].reshape(4 * half, D + EXTRA)
+        four = rows[pl.ds(first * SUBS, 4 * SUBS)].reshape(4 * half, D + EXTRA)
         x = four[:, :D]
         share = jnp.sum(
             jnp.where(chosen, four[:, D:].astype(jnp.float32), 0.0), axis=1, keepdims=True
@@ -410,85 +647,90 @@
 
     def add_line(zb, kind, way):
         to_line(zb, kind, way).wait_recv()
-        side = 1 if way == DOWN else 0
+        side = side_up if way == UPN else 1 - side_up
         acc[...] += from_line[side, zb, kind].astype(jnp.float32)
 
-    def fold(zb, kind):
-        p = min(kind, 1)
-        yb = 1 - y if kind == 2 else y
+    def fold(nb, kind):
+        zb = real(nb)
+        p, yb, b = kind_slot(zb, kind)
         acc[...] = with_twin(zb, p, yb)
-        if kind == 0:
+
+        @pl.when(kind == 0)
+        def _():
             to_pair(zb, 0).wait_recv()
             acc[...] += from_pair[zb].astype(jnp.float32)
-        pl.when((zb > z) & (z > 0))(lambda: add_line(zb, kind, UP))
-        pl.when((zb < z) & (z < LINE - 1))(lambda: add_line(zb, kind, DOWN))
-        part[slot(zb, p, yb, core)] = acc[...].astype(jnp.bfloat16)
-        pl.when(zb > z)(to_line(zb, kind, UP).start)
-        pl.when(zb < z)(to_line(zb, kind, DOWN).start)
-
-    low = z < LINE // 2
-    inner = jnp.where(low, z, LINE - 1 - z)
-
-    def fold_at(j):
-        near = lax.rem(j + 1 + inner, LINE)
-        return jnp.where(low, near, LINE - 1 - near)
-
-    def step(i, carry):
-        @pl.when(i < LINE)
-        def _():
-            zb = place.line_at(i)
-
-            @pl.when(i == 0)
-            def _():
-                b = slot(z, 1, 1 - y, core)
-                gather.wait(b)
-                along(b, z)
-                gather.copy(b, TWIN).start()
-                for load in loads[2:]:
-                    load.wait()
-
-            @pl.when(i > 0)
-            def _():
-                for p, yb in ((1, y), (0, y), (1, 1 - y)):
-                    b = slot(zb, p, yb, core)
-                    gather.wait(b)
-                    if p == 0:
-                        gather.copy(b, ACROSS).start()
-                    along(b, zb)
-                    gather.copy(b, TWIN).start()
-
-            serve(zb, 1)
-
-        @pl.when((i > 0) & (i <= LINE))
-        def _():
-            zb = place.line_at(i - 1)
-            b = slot(zb, 0, 1 - y, core)
-            gather.wait(b)
-            gather.copy(b, TWIN).start()
-            serve(zb, 0)
-
+
+        pl.when((nb > inner) & (inner == 1))(lambda: add_line(zb, kind, UPN))
+        pl.when(nb < inner)(lambda: add_line(zb, kind, DOWNN))
+        part[b] = acc[...].astype(jnp.bfloat16)
+        pl.when(nb > inner)(to_line(zb, kind, UPN).start)
+        pl.when(nb < inner)(to_line(zb, kind, DOWNN).start)
+
+    def happen(code):
+        h = lax.rem(code, 2)
+        piece = lax.rem(code // 2, 4)
+        nb = lax.rem(code // 8, 4)
+        kind = code // 32
+        p = jnp.where(piece <= PB, 1, 0)
+        yb = jnp.where((piece == PA) | (piece == PC), y, 1 - y)
+
+        @pl.when(kind == ARRIVE)
+        def _():
+            b = slot(real(nb), p, yb, core)
+            copy(b, h, TWIN).wait_recv()
+            onward = piece != PD
+            pl.when(onward & (nb < inner))(copy(b, h, UPN).start)
+            pl.when(onward & (nb > inner) & (inner == 1))(copy(b, h, DOWNN).start)
+            pl.when((piece == PC) & (nb != inner))(copy(b, h, ACROSS).start)
+            copy(b, h, TWIN).start()
+
+        mine = slot(z, p, yb, core)
+        pl.when(kind == OWN_UP)(copy(mine, h, UPN).start)
+        pl.when(kind == OWN_DOWN)(copy(mine, h, DOWNN).start)
+
+    end_words = [events(e[0]) for e in END_STEPS]
+    inner_words = [events(e[0]) for e in INNER_STEPS]
+
+    def step(s, carry):
+        for w in range(WORDS):
+            def one(j, word):
+                happen(lax.rem(word, 128))
+                return word // 128
+
+            lax.fori_loop(0, 4, one, pick(s, inner, [e[w] for e in end_words], [e[w] for e in inner_words]))
+
+        @pl.when(s == 0)
+        def _():
+            for load in loads[2 * SUBS :]:
+                load.wait()
+
+        nb = pick(
+            s, inner, [int(e[1][0]) for e in END_STEPS], [int(e[1][0]) for e in INNER_STEPS]
+        )
+        zb = real(nb)
+        p = 1 - lax.rem(s, 2)
+        serve(zb, p)
+
+        @pl.when(p == 0)
+        def _():
             part[slot(zb, 0, 1 - y, core)] = with_twin(zb, 0, 1 - y).astype(jnp.bfloat16)
             to_pair(zb, 0).start()
 
-        late = i - 1 - 2 * inner
-
-        @pl.when((late >= 0) & (late < LINE - 1))
-        def _():
-            zb = fold_at(late)
-            fold(zb, 1)
-            fold(zb, 2)
-
-        @pl.when((late >= 1) & (late < LINE))
-        def _():
-            fold(fold_at(late - 1), 0)
-
+        def one_fold(j, word):
+            code = lax.rem(word, 16)
+            pl.when(code < 15)(lambda: fold(code // 4, lax.rem(code, 4)))
+            return word // 16
+
+        lax.fori_loop(0, 7, one_fold, pick(
+            s, inner, [folds(e[2]) for e in END_STEPS], [folds(e[2]) for e in INNER_STEPS]
+        ))
         return carry
 
-    lax.fori_loop(0, LINE + 3, step, 0)
+    lax.fori_loop(0, len(END_STEPS), step, 0)
 
     def both_sides(kind):
-        pl.when(z > 0)(lambda: add_line(z, kind, UP))
-        pl.when(z < LINE - 1)(lambda: add_line(z, kind, DOWN))
+        pl.when(inner == 1)(lambda: add_line(z, kind, UPN))
+        add_line(z, kind, DOWNN)
 
     acc[...] = with_twin(z, 1, 1 - y)
     both_sides(2)
@@ -501,24 +743,30 @@
         to_pair(z, p).wait_recv()
         acc[...] += from_pair[LINE if p else z].astype(jnp.float32)
         out_ref[here] = acc[...].astype(jnp.bfloat16)
-    gather.copy(slot(z, 1, y, core), ACROSS).wait_send()
+    for h in range(SUBS):
+        copy(own_a, h, ACROSS).wait_send()
     to_pair(z, 1).wait_send()
 
-    def settle(zb, carry):
-        for p, yb in ((0, y), (1, y), (1, 1 - y)):
-            for wanted, way in gather.line_ways(zb):
-                pl.when(wanted)(gather.copy(slot(zb, p, yb, core), way).wait_send)
-        gather.copy(slot(zb, 0, y, core), ACROSS).wait_send()
+    def settle(nb, carry):
+        zb = real(nb)
+        for h in range(SUBS):
+            for p, yb in ((0, y), (1, y), (1, 1 - y)):
+                b = slot(zb, p, yb, core)
+                pl.when(nb <= inner)(copy(b, h, UPN).wait_send)
+                pl.when((nb >= inner) & (inner == 1))(copy(b, h, DOWNN).wait_send)
+            copy(slot(zb, 0, y, core), h, ACROSS).wait_send()
+            for p in range(2):
+                for yb in (y, 1 - y):
+                    copy(slot(zb, p, yb, core), h, TWIN).wait_send()
         for p in range(2):
             for yb in (y, 1 - y):
-                gather.copy(slot(zb, p, yb, core), TWIN).wait_send()
                 to_twin(zb, p, yb).wait_send()
         to_pair(zb, 0).wait_send()
 
-        @pl.when(zb != z)
+        @pl.when(nb != inner)
         def _():
             for kind in range(3):
-                to_line(zb, kind, UP).wait_send()
+                to_line(zb, kind, UPN).wait_send()
 
         return carry
 
@@ -541,7 +789,7 @@
         out_specs=vmem,
         out_shape=jax.ShapeDtypeStruct((tokens, D), jnp.bfloat16),
         scratch_shapes=[
-            pltpu.VMEM((2 * devices, half, x.shape[1]), jnp.bfloat16),
+            pltpu.VMEM((2 * devices * SUBS, half // SUBS, x.shape[1]), jnp.bfloat16),
             held(2 * devices),
             held(devices),
             held(LINE + 1),
@@ -550,15 +798,17 @@
             pltpu.VMEM(gate_w.shape, jnp.bfloat16),
             pltpu.VMEM(up_w.shape, jnp.bfloat16),
             pltpu.VMEM(down_w.shape, jnp.bfloat16),
-            dma((5,)),
-            dma((2 * devices, 4)),
-            dma((2 * devices,)),
+            dma((2 * SUBS + 3,)),
+            dma((2 * devices * SUBS, 4)),
+            dma((2 * devices * SUBS,)),
             dma((2 * devices,)),
             dma((devices,)),
             dma((LINE + 1,)),
             dma((2, LINE, 3)),
         ],
-        compiler_params=pltpu.CompilerParams(collective_id=1, has_side_effects=True),
+        compiler_params=pltpu.CompilerParams(
+            collective_id=1, has_side_effects=True, vmem_limit_bytes=60 << 20
+        ),
     )(x, gate_w, up_w, down_w, mixed)
 
 
@@ -620,7 +870,7 @@
     weights = P("wide", None, None)
     placed = (rows, rows, rows, rows, blocks, blocks, P("groups"), P("wide", None), P())
     placed += (rows, rows, weights, weights, weights)
-    grid = mesh.shape["wide"] == LINE * PAIR * 2
+    grid = mesh.shape["wide"] == LINE * PAIR * 2 and mesh.shape["groups"] == 2
     return jax.shard_map(
         grid_device if grid else per_device,
         mesh=mesh,

time: 192 us -> 172 us (0.90)
  Pallas kernels: 187 us -> 167 us
    pallas_call x1, Pallas kernels: 62.1 us -> 45.3 us  [attention_block(): pl.pallas_call(attention_block_kernel, in_specs=[pl.BlockSpec(memory_spac...]
    pallas_call x1, Pallas kernels: 125 us -> 122 us  [experts_block(): pl.pallas_call(experts_kernel, in_specs=[whole] * 4 + [vmem], out_specs=v...]
where the time goes in v1:
time: 172 us
  Pallas kernels  167 us (97%)
  local copies, waits for them, and re-layouts  2.63 us (2%)
  other arithmetic  2.11 us (1%)
    pallas_call x1, Pallas kernels, experts_block(): pl.pallas_call(experts_kernel, in_specs=[whole] * 4 + [vmem], out_specs=v...  122 us
    pallas_call x1, Pallas kernels, attention_block(): pl.pallas_call(attention_block_kernel, in_specs=[pl.BlockSpec(memory_spac...  45.3 us

profile of v1, /device:TPU:0, one launch (start us, length us, event | category | flops | bytes accessed | tf_op | source)
XLA Modules:
  0.0 172.1 jit_solution(1049711922737539900)
XLA Ops:
  0.0 0.7 reduce_sum.18
  0.7 0.7 broadcast_divide_fusion
  1.4 0.7 select_reduce_fusion
  2.1 0.1 copy.20
  2.2 0.6 pad.4.extra_ref
  2.9 45.3 %shard_map.136 = (f32[128,2048]{1,0:T(8,128)}, bf16[128,2176]{1,0:T(8,128)(2,1)}) custom-call(s32[16]{0:T(128)} %length_ref.1, bf16[128,2048]{1,0:T(8,128)(2,1)} %q_ref.1, bf16[128,256]{1,0:T(8,128)(2,1)} %nk_ref.1, bf16[128,256]{1,0:T(8,128)(2,1)} %nv_ref.1, bf16[1,2048,256]{2,1,0:T(8,128)(2,1)} %k_ref.1, bf16[1,2048,256]{2,1,0:T(8,128)(2,1)} %v_ref.1, ...), custom_call_target="tpu_custom_call" | custom-call | tf_op jit(solution)/shard_map/pallas_call | solution.py:449
  48.2 122.1 %shard_map.137 = bf16[128,2048]{1,0:T(8,128)(2,1)} custom-call(bf16[128,2176]{1,0:T(8,128)(2,1)} %get-tuple-element.7.x_ref, bf16[2048,768]{1,0:T(8,128)(2,1)} %bitcast.4, bf16[2048,768]{1,0:T(8,128)(2,1)} %bitcast.5, bf16[768,2048]{1,0:T(8,128)(2,1)} %bitcast.6, f32[128,2048]{1,0:T(8,128)} %get-tuple-element.8.mixed_ref), custom_call_target="tpu_custom_call" | custom-call | tf_op jit(solution)/shard_map/pallas_call | solution.py:786
  170.2 1.9 %copy.22 = bf16[128,2048]{1,0:T(8,128)(2,1)} copy(bf16[128,2048]{1,0:T(8,128)(2,1)} %shard_map.137) | data formatting | bytes 1048576
  (2 shorter events, 0.0 us)

commit v2 on v1

--- a/solution.py
+++ b/solution.py
@@ -100,7 +100,6 @@
 
 LINE = 4
 PAIR = 2
-EXTRA = 128
 DOWN, UP, ACROSS, TWIN = range(4)
 
 
@@ -178,6 +177,7 @@
 TILE = 16
 P0, P1, PR, Q0, Q1, QS = range(6)
 A_SLOTS = 6
+SHARE_ROWS = 32
 
 
 def gather_events(*items):
@@ -220,9 +220,54 @@
     return jnp.where(inner == 1, at_inner, at_end)
 
 
-def attention_block_kernel(
-    length_ref, q_ref, nk_ref, nv_ref, k_ref, v_ref, res_ref, gain_ref, extra_ref, ow_ref,
-    mixed_ref, rows_ref, held, attn, own_sem, send_sem, recv_sem,
+PIECES = "abcd"
+GET, UP_OWN, DOWN_OWN, PASS_OWN, SERVE, PAIR_UP, FOLD, FINISH = range(8)
+KINDS = {"g": GET, "u": UP_OWN, "d": DOWN_OWN, "y": PASS_OWN}
+KINDS.update({"s": SERVE, "p": PAIR_UP, "f": FOLD, "z": FINISH})
+PA, PB, PC, PD = range(4)
+B_END = (
+    "uc", "ua", "ya", "yc", "g0b", "ub", "g1b", "g1a", "s11", "g3c", "g0d", "s00",
+    "g3d", "g3a", "f11", "s30", "f12", "g3b", "p0", "p3", "s31", "f32", "f31", "s01",
+    "g2c", "g2a", "f30", "g2b", "s21", "g2d", "g1c", "f22", "s20", "f21", "g1d", "p2",
+    "s10", "p1", "f20", "z2", "f10", "z0", "z1",
+)
+B_INNER = (
+    "ya", "uc", "da", "g0c", "g1b", "db", "g0a", "yc", "g3c", "g0b", "g3a", "s11",
+    "ua", "g0d", "g3b", "g2c", "g1d", "s31", "ub", "g2a", "g3d", "s30", "s00", "g2b",
+    "p3", "dc", "s10", "p0", "f32", "s21", "f31", "p1", "s01", "g2d", "f30", "f02",
+    "s20", "f22", "p2", "f01", "f21", "f00", "z2", "f20", "z1", "z0",
+)
+
+
+def code_of(text):
+    kind = KINDS[text[0]]
+    if kind == GET:
+        return kind * 16 + int(text[1]) * 4 + PIECES.index(text[2])
+    if kind in (UP_OWN, DOWN_OWN, PASS_OWN):
+        return kind * 16 + PIECES.index(text[1])
+    if kind == PAIR_UP:
+        return kind * 16 + int(text[1]) * 4
+    if kind == FINISH:
+        return kind * 16 + int(text[1])
+    return kind * 16 + int(text[1]) * 4 + int(text[2])
+
+
+def packed(program, words):
+    codes = [code_of(text) for text in program]
+    codes += [127] * (4 * words - len(codes))
+    return [sum(c << (7 * j) for j, c in enumerate(codes[4 * w : 4 * w + 4])) for w in range(words)]
+
+
+def first_serve(program):
+    return [text[0] for text in program].index("s")
+
+
+def layer_kernel(
+    length_ref, q_ref, nk_ref, nv_ref, k_ref, v_ref, res_ref, gain_ref, share_ref, ow_ref,
+    wg_ref, wu_ref, wd_ref, out_ref,
+    held, attn, mixed_ref, share_tab, share_col, rows, part, from_twin, from_pair, from_line, acc,
+    wg, wu, wd, own_sem, load_sem, send_sem, recv_sem, share_send, share_recv,
+    row_send, row_recv, back_send, twin_sem, pair_sem, line_sem,
 ):
     place = Place()
     z, y, core = place.z, place.y, place.core
@@ -234,6 +279,13 @@
     step_up = jnp.where(low, 1, -1)
     own = pltpu.make_async_copy(ow_ref, held.at[place.me], own_sem)
     own.start()
+    loads = [
+        pltpu.make_async_copy(source, dest, load_sem.at[k])
+        for k, (source, dest) in enumerate(((wg_ref, wg), (wu_ref, wu), (wd_ref, wd)))
+    ]
+    for load in loads:
+        load.start()
+    share_tab[place.me] = share_ref[...]
     place.barrier(True)
     own.wait()
 
@@ -280,6 +332,13 @@
             device_id_type=pl.DeviceIdType.MESH,
         )
 
+    def share_copy(b, way):
+        return pltpu.make_async_remote_copy(
+            src_ref=share_tab.at[b], dst_ref=share_tab.at[b], send_sem=share_send.at[b, way],
+            recv_sem=share_recv.at[b], device_id=device(way),
+            device_id_type=pl.DeviceIdType.MESH,
+        )
+
     def block_at(nb, yb, c):
         return place.block(real(nb), yb, c)
 
@@ -291,6 +350,10 @@
     pl.when(inner == 1)(copy(me, P1, DOWNN).start)
     copy(me, Q1, ACROSS).start()
     whole(me).start()
+    share_copy(me, UPN).start()
+    pl.when(inner == 1)(share_copy(me, DOWNN).start)
+    share_copy(me, ACROSS).start()
+    share_copy(me, TWIN).start()
 
     def happen(code):
         nb = lax.rem(code, 4)
@@ -309,6 +372,11 @@
             copy(own_b, Q0, ACROSS).start()
             copy(own_b, PR, XWAY).start()
             copy(own_b, P0, TWIN).start()
+            share_copy(own_b, TWIN).wait_recv()
+            pl.when(nb < inner)(share_copy(own_b, UPN).start)
+            pl.when((nb > inner) & (inner == 1))(share_copy(own_b, DOWNN).start)
+            share_copy(own_b, ACROSS).start()
+            share_copy(own_b, TWIN).start()
 
         @pl.when(kind == P1)
         def _():
@@ -327,6 +395,8 @@
             copy(other_b, Q0, TWIN).wait_recv()
             copy(other_b, QS, XWAY).start()
             copy(other_b, Q0, TWIN).start()
+            share_copy(other_b, TWIN).wait_recv()
+            share_copy(other_b, TWIN).start()
 
         @pl.when(kind == Q1)
         def _():
@@ -361,6 +431,8 @@
             ]
 
     mixed_ref[...] = res_ref[...].astype(jnp.float32)
+    lane = lax.broadcasted_iota(jnp.int32, (1, SHARE_ROWS), 1)
+    chosen = (lane == me) | (lane == me + SHARE_ROWS // 2)
 
     def project(nb, is_own):
         yb = jnp.where(is_own, y, 1 - y)
@@ -380,10 +452,15 @@
             for what in (Q0, Q1, QS):
                 copy(b, what, TWIN).wait_recv()
 
+        share_copy(b, TWIN).wait_recv()
         first = block_at(nb, yb, 0)
-        part = attn[:, pl.ds(pl.multiple_of(first * depth, 2 * depth), 2 * depth)]
+        for c in range(2):
+            turned = share_tab[first + c].astype(jnp.float32).T
+            column = jnp.sum(jnp.where(chosen, turned, 0.0), axis=1, keepdims=True)
+            share_col[first + c] = jnp.broadcast_to(column, share_col.shape[1:])
+        mine = attn[:, pl.ds(pl.multiple_of(first * depth, 2 * depth), 2 * depth)]
         weight = held[pl.ds(first, 2)].reshape(2 * depth, D)
-        mixed_ref[...] += jnp.dot(part, weight, preferred_element_type=jnp.float32)
+        mixed_ref[...] += jnp.dot(mine, weight, preferred_element_type=jnp.float32)
 
     def step(s, carry):
         def one(j, word):
@@ -407,193 +484,25 @@
         return carry
 
     lax.fori_loop(0, len(A_END), step, 0)
+    half_rows = tokens // 2
     mixed = mixed_ref[...]
     scale = lax.rsqrt(jnp.mean(mixed * mixed, axis=-1, keepdims=True) + 1e-06)
-    rows_ref[:, :D] = (mixed * scale * gain_ref[...]).astype(jnp.bfloat16)
-    rows_ref[:, D:] = extra_ref[...]
-
-    def settle(nb, carry):
-        own_b = block_at(nb, y, core)
-        other_b = block_at(nb, 1 - y, core)
-        for what in (P0, P1):
-            pl.when(nb <= inner)(copy(own_b, what, UPN).wait_send)
-            pl.when((nb >= inner) & (inner == 1))(copy(own_b, what, DOWNN).wait_send)
-        copy(own_b, Q0, ACROSS).wait_send()
-        copy(own_b, Q1, ACROSS).wait_send()
-
-        @pl.when(nb == inner)
-        def _():
-            whole(own_b).wait_send()
-
-        @pl.when(nb != inner)
-        def _():
-            copy(own_b, PR, XWAY).wait_send()
-            for what in (P0, P1, PR):
-                copy(own_b, what, TWIN).wait_send()
-
-        copy(other_b, QS, XWAY).wait_send()
-        for what in (Q0, Q1, QS):
-            copy(other_b, what, TWIN).wait_send()
-        return carry
-
-    lax.fori_loop(0, LINE, settle, 0)
-
-
-def attention_block(
-    cache_len, queries, new_keys, new_values, cache_keys, cache_values, residual, gain, extra,
-    o_weight, devices,
-):
-    tokens, width = queries.shape
-    cache = cache_keys.shape[1]
-    vmem = pl.BlockSpec(memory_space=pltpu.VMEM)
-    return pl.pallas_call(
-        attention_block_kernel,
-        in_specs=[pl.BlockSpec(memory_space=pltpu.SMEM)] + [vmem] * 8
-        + [pl.BlockSpec(memory_space=pl.ANY)],
-        out_specs=[vmem, vmem],
-        out_shape=[
-            jax.ShapeDtypeStruct((tokens, D), jnp.float32),
-            jax.ShapeDtypeStruct((tokens, D + EXTRA), jnp.bfloat16),
-        ],
-        scratch_shapes=[
-            pltpu.VMEM((devices,) + o_weight.shape, jnp.bfloat16),
-            pltpu.VMEM((tokens, width), jnp.bfloat16),
-            pltpu.SemaphoreType.DMA,
-            pltpu.SemaphoreType.DMA((devices, 3, 5)),
-            pltpu.SemaphoreType.DMA((devices, 3)),
-        ],
-        compiler_params=pltpu.CompilerParams(
-            collective_id=0, has_side_effects=True, vmem_limit_bytes=60 << 20
-        ),
-    )(
-        cache_len, queries, new_keys, new_values, cache_keys, cache_values, residual, gain, extra,
-        o_weight,
-    )
-
-
-SUBS = 2
-PA, PB, PC, PD = range(4)
-ARRIVE, OWN_UP, OWN_DOWN, NOTHING = range(4)
-WORDS = 3
-
-
-def event(kind, nb, piece, h):
-    return ((kind * 4 + nb) * 4 + piece) * 2 + h
-
-
-def events(text):
-    kinds = {"u": OWN_UP, "d": OWN_DOWN}
-    codes = []
-    for item in (text[k : k + 3] for k in range(0, len(text), 3)):
-        if item[0] in kinds:
-            codes.append(event(kinds[item[0]], 0, "abcd".index(item[1]), int(item[2])))
-        else:
-            codes.append(event(ARRIVE, int(item[0]), "abcd".index(item[1]), int(item[2])))
-    assert len(codes) <= 4 * WORDS
-    codes += [127] * (4 * WORDS - len(codes))
-    return [sum(c << (7 * j) for j, c in enumerate(codes[4 * w : 4 * w + 4])) for w in range(WORDS)]
-
-
-def folds(text):
-    codes = [int(item[0]) * 4 + int(item[1]) for item in (text[k : k + 2] for k in range(0, len(text), 2))]
-    codes += [15] * (7 - len(codes))
-    return sum(c << (4 * j) for j, c in enumerate(codes))
-
-
-END_STEPS = (
-    ("0b0ub00b1ub1uc0uc11a0", "01", ""),
-    ("0d00d12a0", "00", ""),
-    ("3a03a13b03b1", "31", "3132"),
-    ("3c03c13d03d1", "30", ""),
-    ("2a12b02b1", "21", "302122"),
-    ("2c02c12d02d1", "20", ""),
-    ("1a11b01b1", "11", "201112"),
-    ("1c01c11d01d1", "10", "10"),
-)
-INNER_STEPS = (
-    ("0a02a01b00a13a01b1", "11", ""),
-    ("0b03a11d00b13b01d1", "10", ""),
-    ("0c03b10c13c0ua1ub0ub1uc0uc1", "01", ""),
-    ("3c10d00d1", "00", ""),
-    ("2a1da1db0", "31", ""),
-    ("2b03d03d12b1db1", "30", ""),
-    ("2c02c1dc0dc1", "21", "3132"),
-    ("2d02d1", "20", "30010221002220"),
-)
-
-
-def experts_kernel(
-    x_ref, wg_ref, wu_ref, wd_ref, mixed_ref, out_ref,
-    rows, part, from_twin, from_pair, from_line, acc, wg, wu, wd,
-    own_sem, send_sem, recv_sem, back_send, twin_sem, pair_sem, line_sem,
-):
-    place = Place()
-    me, z, y, core = place.me, place.z, place.y, place.core
-    half = x_ref.shape[0] // 2
-    sub = half // SUBS
-    devices = rows.shape[0] // (2 * SUBS)
-    low = z < LINE // 2
-    inner = jnp.where(low, z, LINE - 1 - z)
-    step_up = jnp.where(low, 1, -1)
-    side_up = jnp.where(low, 0, 1)
-
-    def real(nb):
-        return jnp.where(low, nb, LINE - 1 - nb)
-
-    def target(way):
-        if way == UPN:
-            return place.block(z + step_up, y, core)
-        if way == DOWNN:
-            return place.block(z - step_up, y, core)
-        return place.towards(way)
+    normed = (mixed * scale * gain_ref[...]).astype(jnp.bfloat16)
+
+    def slot(zb, p, yb, c):
+        return ((zb * 2 + p) * PAIR + yb) * 2 + c
+
+    for p in range(2):
+        rows[slot(z, p, y, core)] = normed[p * half_rows : (p + 1) * half_rows]
 
     def send(source, dest, send_one, recv_one, way):
         return pltpu.make_async_remote_copy(
             src_ref=source, dst_ref=dest, send_sem=send_one, recv_sem=recv_one,
-            device_id={"wide": target(way)}, device_id_type=pl.DeviceIdType.MESH,
+            device_id=device(way), device_id_type=pl.DeviceIdType.MESH,
         )
 
-    def slot(zb, p, yb, c):
-        return ((zb * 2 + p) * PAIR + yb) * 2 + c
-
-    def copy(b, h, way):
-        t = b * SUBS + h
-        return send(rows.at[t], rows.at[t], send_sem.at[t, way], recv_sem.at[t], way)
-
-    loads = [
-        pltpu.make_async_copy(
-            x_ref.at[pl.ds(p * half + h * sub, sub)],
-            rows.at[slot(z, p, y, core) * SUBS + h],
-            own_sem.at[p * SUBS + h],
-        )
-        for p in range(2)
-        for h in range(SUBS)
-    ]
-    loads += [
-        pltpu.make_async_copy(source, dest, own_sem.at[2 * SUBS + k])
-        for k, (source, dest) in enumerate(((wg_ref, wg), (wu_ref, wu), (wd_ref, wd)))
-    ]
-    for load in loads:
-        load.start()
-    place.barrier()
-    own_a = slot(z, 1, y, core)
-    own_c = slot(z, 0, y, core)
-    for h in range(SUBS):
-        loads[SUBS + h].wait()
-        copy(own_a, h, ACROSS).start()
-        if h == 0:
-            copy(own_a, h, UPN).start()
-            pl.when(inner == 1)(copy(own_a, h, DOWNN).start)
-        else:
-            pl.when(inner == 0)(copy(own_a, h, UPN).start)
-        copy(own_a, h, TWIN).start()
-    for h in range(SUBS):
-        loads[h].wait()
-        copy(own_c, h, ACROSS).start()
-        copy(own_c, h, TWIN).start()
-
-    lane = lax.broadcasted_iota(jnp.int32, (1, EXTRA), 1)
-    chosen = (lane == me) | (lane == me + devices)
+    def row_copy(b, way):
+        return send(rows.at[b], rows.at[b], row_send.at[b, way], row_recv.at[b], way)
 
     def to_twin(zb, p, yb):
         b = slot(zb, p, yb, 1 - core)
@@ -609,6 +518,8 @@
         p = jnp.minimum(kind, 1)
         yb = jnp.where(kind == 2, 1 - y, y)
         return p, yb, slot(zb, p, yb, core)
+
+    side_up = jnp.where(low, 0, 1)
 
     def to_line(zb, kind, way):
         b = kind_slot(zb, kind)[2]
@@ -618,24 +529,18 @@
             line_sem.at[side, zb, kind], way,
         )
 
-    def wait_rows(b):
-        for h in range(SUBS):
-            copy(b, h, TWIN).wait_recv()
-
     def serve(zb, p):
-        wait_rows(slot(zb, p, 0, 1 - core))
-        wait_rows(slot(zb, p, 1, 1 - core))
+        for yb in range(2):
+            row_copy(slot(zb, p, yb, 1 - core), TWIN).wait_recv()
         first = slot(zb, p, 0, 0)
-        four = rows[pl.ds(first * SUBS, 4 * SUBS)].reshape(4 * half, D + EXTRA)
-        x = four[:, :D]
-        share = jnp.sum(
-            jnp.where(chosen, four[:, D:].astype(jnp.float32), 0.0), axis=1, keepdims=True
-        )
+        x = rows[pl.ds(first, 4)].reshape(4 * half_rows, D)
+        here = pl.ds(pl.multiple_of(p * half_rows, half_rows), half_rows)
+        share = share_col[pl.ds(place.block(zb, 0, 0), 4), here].reshape(4 * half_rows, HEAD)
         gate = jnp.dot(x, wg[...], preferred_element_type=jnp.float32)
         up = jnp.dot(x, wu[...], preferred_element_type=jnp.float32)
         act = (gate / (1.0 + jnp.exp(-gate)) * up).astype(jnp.bfloat16)
-        out = jnp.dot(act, wd[...], preferred_element_type=jnp.float32) * share
-        part[pl.ds(first, 4)] = out.astype(jnp.bfloat16).reshape(4, half, D)
+        out = jnp.dot(act, wd[...], preferred_element_type=jnp.float32) * share[:, :1]
+        part[pl.ds(first, 4)] = out.astype(jnp.bfloat16).reshape(4, half_rows, D)
         to_twin(zb, p, 0).start()
         to_twin(zb, p, 1).start()
 
@@ -666,102 +571,99 @@
         pl.when(nb > inner)(to_line(zb, kind, UPN).start)
         pl.when(nb < inner)(to_line(zb, kind, DOWNN).start)
 
-    def happen(code):
-        h = lax.rem(code, 2)
-        piece = lax.rem(code // 2, 4)
-        nb = lax.rem(code // 8, 4)
-        kind = code // 32
+    def finish(kind):
+        p, yb, b = kind_slot(z, kind)
+        acc[...] = with_twin(z, p, yb)
+        pl.when(inner == 1)(lambda: add_line(z, kind, UPN))
+        add_line(z, kind, DOWNN)
+
+        @pl.when(kind == 2)
+        def _():
+            part[b] = acc[...].astype(jnp.bfloat16)
+            to_pair(z, 1).start()
+
+        def close(p, t):
+            here = pl.ds(p * half_rows, half_rows)
+            to_pair(z, p).wait_recv()
+            out_ref[here] = (
+                acc[...] + mixed_ref[here] + from_pair[t].astype(jnp.float32)
+            ).astype(jnp.bfloat16)
+
+        pl.when(kind == 0)(lambda: close(0, z))
+        pl.when(kind == 1)(lambda: close(1, LINE))
+
+    def act_on(code, first):
+        kind = code // 16
+        nb = lax.rem(code // 4, 4)
+        piece = lax.rem(code, 4)
+        zb = real(nb)
         p = jnp.where(piece <= PB, 1, 0)
         yb = jnp.where((piece == PA) | (piece == PC), y, 1 - y)
-
-        @pl.when(kind == ARRIVE)
-        def _():
-            b = slot(real(nb), p, yb, core)
-            copy(b, h, TWIN).wait_recv()
+        own_piece = slot(z, p, yb, core)
+
+        @pl.when(kind == GET)
+        def _():
+            b = slot(zb, p, yb, core)
+            row_copy(b, TWIN).wait_recv()
             onward = piece != PD
-            pl.when(onward & (nb < inner))(copy(b, h, UPN).start)
-            pl.when(onward & (nb > inner) & (inner == 1))(copy(b, h, DOWNN).start)
-            pl.when((piece == PC) & (nb != inner))(copy(b, h, ACROSS).start)
-            copy(b, h, TWIN).start()
-
-        mine = slot(z, p, yb, core)
-        pl.when(kind == OWN_UP)(copy(mine, h, UPN).start)
-        pl.when(kind == OWN_DOWN)(copy(mine, h, DOWNN).start)
-
-    end_words = [events(e[0]) for e in END_STEPS]
-    inner_words = [events(e[0]) for e in INNER_STEPS]
-
-    def step(s, carry):
-        for w in range(WORDS):
-            def one(j, word):
-                happen(lax.rem(word, 128))
-                return word // 128
-
-            lax.fori_loop(0, 4, one, pick(s, inner, [e[w] for e in end_words], [e[w] for e in inner_words]))
-
-        @pl.when(s == 0)
-        def _():
-            for load in loads[2 * SUBS :]:
-                load.wait()
-
-        nb = pick(
-            s, inner, [int(e[1][0]) for e in END_STEPS], [int(e[1][0]) for e in INNER_STEPS]
-        )
-        zb = real(nb)
-        p = 1 - lax.rem(s, 2)
-        serve(zb, p)
-
-        @pl.when(p == 0)
+            pl.when(onward & (nb < inner))(row_copy(b, UPN).start)
+            pl.when(onward & (nb > inner) & (inner == 1))(row_copy(b, DOWNN).start)
+            pl.when((piece == PC) & (nb != inner))(row_copy(b, ACROSS).start)
+            row_copy(b, TWIN).start()
+
+        pl.when(kind == UP_OWN)(row_copy(own_piece, UPN).start)
+        pl.when(kind == DOWN_OWN)(row_copy(own_piece, DOWNN).start)
+
+        @pl.when(kind == PASS_OWN)
+        def _():
+            row_copy(own_piece, ACROSS).start()
+            row_copy(own_piece, TWIN).start()
+
+        @pl.when(kind == SERVE)
+        def _():
+            @pl.when(first)
+            def _():
+                for load in loads:
+                    load.wait()
+
+            serve(zb, piece)
+
+        @pl.when(kind == PAIR_UP)
         def _():
             part[slot(zb, 0, 1 - y, core)] = with_twin(zb, 0, 1 - y).astype(jnp.bfloat16)
             to_pair(zb, 0).start()
 
-        def one_fold(j, word):
-            code = lax.rem(word, 16)
-            pl.when(code < 15)(lambda: fold(code // 4, lax.rem(code, 4)))
-            return word // 16
-
-        lax.fori_loop(0, 7, one_fold, pick(
-            s, inner, [folds(e[2]) for e in END_STEPS], [folds(e[2]) for e in INNER_STEPS]
-        ))
+        pl.when(kind == FOLD)(lambda: fold(nb, piece))
+        pl.when((kind == FINISH) & (piece < 3))(lambda: finish(piece))
+
+    words = -(-max(len(B_END), len(B_INNER)) // 4)
+    end_words, inner_words = packed(B_END, words), packed(B_INNER, words)
+    serve_at = jnp.where(inner == 1, first_serve(B_INNER), first_serve(B_END))
+
+    def route(w, carry):
+        def one(j, word):
+            act_on(lax.rem(word, 128), w * 4 + j == serve_at)
+            return word // 128
+
+        lax.fori_loop(0, 4, one, pick(w, inner, end_words, inner_words))
         return carry
 
-    lax.fori_loop(0, len(END_STEPS), step, 0)
-
-    def both_sides(kind):
-        pl.when(inner == 1)(lambda: add_line(z, kind, UPN))
-        add_line(z, kind, DOWNN)
-
-    acc[...] = with_twin(z, 1, 1 - y)
-    both_sides(2)
-    part[slot(z, 1, 1 - y, core)] = acc[...].astype(jnp.bfloat16)
-    to_pair(z, 1).start()
-    for p in range(2):
-        here = pl.ds(p * half, half)
-        acc[...] = with_twin(z, p, y) + mixed_ref[here]
-        both_sides(p)
-        to_pair(z, p).wait_recv()
-        acc[...] += from_pair[LINE if p else z].astype(jnp.float32)
-        out_ref[here] = acc[...].astype(jnp.bfloat16)
-    for h in range(SUBS):
-        copy(own_a, h, ACROSS).wait_send()
-    to_pair(z, 1).wait_send()
-
-    def settle(nb, carry):
+    lax.fori_loop(0, words, route, 0)
+
+    def settle_rows(nb, carry):
         zb = real(nb)
-        for h in range(SUBS):
-            for p, yb in ((0, y), (1, y), (1, 1 - y)):
-                b = slot(zb, p, yb, core)
-                pl.when(nb <= inner)(copy(b, h, UPN).wait_send)
-                pl.when((nb >= inner) & (inner == 1))(copy(b, h, DOWNN).wait_send)
-            copy(slot(zb, 0, y, core), h, ACROSS).wait_send()
-            for p in range(2):
-                for yb in (y, 1 - y):
-                    copy(slot(zb, p, yb, core), h, TWIN).wait_send()
+        for p, yb in ((0, y), (1, y), (1, 1 - y)):
+            b = slot(zb, p, yb, core)
+            pl.when(nb <= inner)(row_copy(b, UPN).wait_send)
+            pl.when((nb >= inner) & (inner == 1))(row_copy(b, DOWNN).wait_send)
+        row_copy(slot(zb, 0, y, core), ACROSS).wait_send()
+        pl.when(nb == inner)(row_copy(slot(zb, 1, y, core), ACROSS).wait_send)
         for p in range(2):
             for yb in (y, 1 - y):
+                row_copy(slot(zb, p, yb, core), TWIN).wait_send()
                 to_twin(zb, p, yb).wait_send()
         to_pair(zb, 0).wait_send()
+        pl.when(nb == inner)(to_pair(zb, 1).wait_send)
 
         @pl.when(nb != inner)
         def _():
@@ -770,26 +672,65 @@
 
         return carry
 
-    lax.fori_loop(0, LINE, settle, 0)
-
-
-def experts_block(x, gate_w, up_w, down_w, mixed, devices):
-    tokens = x.shape[0]
+    lax.fori_loop(0, LINE, settle_rows, 0)
+
+    def settle_weights(nb, carry):
+        own_b = block_at(nb, y, core)
+        other_b = block_at(nb, 1 - y, core)
+        for what in (P0, P1):
+            pl.when(nb <= inner)(copy(own_b, what, UPN).wait_send)
+            pl.when((nb >= inner) & (inner == 1))(copy(own_b, what, DOWNN).wait_send)
+        pl.when(nb <= inner)(share_copy(own_b, UPN).wait_send)
+        pl.when((nb >= inner) & (inner == 1))(share_copy(own_b, DOWNN).wait_send)
+        share_copy(own_b, ACROSS).wait_send()
+        share_copy(own_b, TWIN).wait_send()
+        share_copy(other_b, TWIN).wait_send()
+        copy(own_b, Q0, ACROSS).wait_send()
+        copy(own_b, Q1, ACROSS).wait_send()
+
+        @pl.when(nb == inner)
+        def _():
+            whole(own_b).wait_send()
+
+        @pl.when(nb != inner)
+        def _():
+            copy(own_b, PR, XWAY).wait_send()
+            for what in (P0, P1, PR):
+                copy(own_b, what, TWIN).wait_send()
+
+        copy(other_b, QS, XWAY).wait_send()
+        for what in (Q0, Q1, QS):
+            copy(other_b, what, TWIN).wait_send()
+        return carry
+
+    lax.fori_loop(0, LINE, settle_weights, 0)
+
+
+def layer(
+    cache_len, queries, new_keys, new_values, cache_keys, cache_values, residual, gain, shares,
+    o_weight, gate_w, up_w, down_w, devices,
+):
+    tokens, width = queries.shape
     half = tokens // 2
     vmem = pl.BlockSpec(memory_space=pltpu.VMEM)
     whole = pl.BlockSpec(memory_space=pl.ANY)
+    dma = pltpu.SemaphoreType.DMA
 
     def held(*lead):
         return pltpu.VMEM(lead + (half, D), jnp.bfloat16)
 
-    dma = pltpu.SemaphoreType.DMA
     return pl.pallas_call(
-        experts_kernel,
-        in_specs=[whole] * 4 + [vmem],
+        layer_kernel,
+        in_specs=[pl.BlockSpec(memory_space=pltpu.SMEM)] + [vmem] * 8 + [whole] * 4,
         out_specs=vmem,
         out_shape=jax.ShapeDtypeStruct((tokens, D), jnp.bfloat16),
         scratch_shapes=[
-            pltpu.VMEM((2 * devices * SUBS, half // SUBS, x.shape[1]), jnp.bfloat16),
+            pltpu.VMEM((devices,) + o_weight.shape, jnp.bfloat16),
+            pltpu.VMEM((tokens, width), jnp.bfloat16),
+            pltpu.VMEM((tokens, D), jnp.float32),
+            pltpu.VMEM((devices,) + shares.shape, jnp.bfloat16),
+            pltpu.VMEM((devices, tokens, HEAD), jnp.float32),
+            held(2 * devices),
             held(2 * devices),
             held(devices),
             held(LINE + 1),
@@ -798,18 +739,26 @@
             pltpu.VMEM(gate_w.shape, jnp.bfloat16),
             pltpu.VMEM(up_w.shape, jnp.bfloat16),
             pltpu.VMEM(down_w.shape, jnp.bfloat16),
-            dma((2 * SUBS + 3,)),
-            dma((2 * devices * SUBS, 4)),
-            dma((2 * devices * SUBS,)),
+            dma,
+            dma((3,)),
+            dma((devices, 3, 5)),
+            dma((devices, 3)),
+            dma((devices, 4)),
+            dma((devices,)),
+            dma((2 * devices, 4)),
+            dma((2 * devices,)),
             dma((2 * devices,)),
             dma((devices,)),
             dma((LINE + 1,)),
             dma((2, LINE, 3)),
         ],
         compiler_params=pltpu.CompilerParams(
-            collective_id=1, has_side_effects=True, vmem_limit_bytes=60 << 20
+            collective_id=0, has_side_effects=True, vmem_limit_bytes=63 << 20
         ),
-    )(x, gate_w, up_w, down_w, mixed)
+    )(
+        cache_len, queries, new_keys, new_values, cache_keys, cache_values, residual, gain, shares,
+        o_weight, gate_w, up_w, down_w,
+    )
 
 
 def grid_device(
@@ -817,17 +766,16 @@
     norm_gain, expert_ids, gate_raw, w_gate, w_up, w_down,
 ):
     devices = lax.axis_size("wide")
-    shares = gate_raw / jnp.sum(gate_raw, axis=-1, keepdims=True)
+    parts = gate_raw / jnp.sum(gate_raw, axis=-1, keepdims=True)
     hits = expert_ids[:, :, None] == jnp.arange(devices, dtype=jnp.int32)[None, None, :]
-    share_of = jnp.sum(jnp.where(hits, shares[..., None], 0.0), axis=1)
+    share_of = jnp.sum(jnp.where(hits, parts[..., None], 0.0), axis=1)
     coarse = share_of.astype(jnp.bfloat16)
     fine = (share_of - coarse.astype(jnp.float32)).astype(jnp.bfloat16)
-    extra = jnp.pad(jnp.concatenate([coarse, fine], axis=1), ((0, 0), (0, EXTRA - 2 * devices)))
-    mixed, rows = attention_block(
+    shares = jnp.concatenate([coarse, fine], axis=1).T
+    return layer(
         cache_len, queries, new_keys, new_values, cache_keys, cache_values, residual,
-        norm_gain.reshape(1, D), extra, o_weight, devices,
+        norm_gain.reshape(1, D), shares, o_weight, w_gate[0], w_up[0], w_down[0], devices,
     )
-    return experts_block(rows, w_gate[0], w_up[0], w_down[0], mixed, devices)
 
 
 def per_device(

time: 172 us -> 141 us (0.82)
  Pallas kernels: 167 us -> 136 us
    pallas_call x2 -> x1, Pallas kernels: 167 us -> 136 us  [layer(): pl.pallas_call(layer_kernel, in_specs=[pl.BlockSpec(memory_space=pltpu.SM...]
where the time goes in v2:
time: 141 us; the launch traced here: 140 us
  Pallas kernels  136 us (96%)
  other arithmetic  2.7 us (2%)
  local copies, waits for them, and re-layouts  1.88 us (1%)
    pallas_call x1, Pallas kernels, layer(): pl.pallas_call(layer_kernel, in_specs=[pl.BlockSpec(memory_space=pltpu.SM...  136 us

profile of v2, /device:TPU:0, one launch (start us, length us, event | category | flops | bytes accessed | tf_op | source)
XLA Modules:
  0.0 140.1 jit_solution(10886210198491368004)
XLA Ops:
  0.0 0.7 reduce_sum.18
  0.7 0.7 broadcast_divide_fusion
  1.4 0.7 select_reduce_fusion
  2.1 0.6 maximum_bitcast_fusion.share_ref
  2.7 135.5 %shard_map.136 = bf16[128,2048]{1,0:T(8,128)(2,1)} custom-call(s32[16]{0:T(128)} %length_ref.1, bf16[128,2048]{1,0:T(8,128)(2,1)} %q_ref.1, bf16[128,256]{1,0:T(8,128)(2,1)} %nk_ref.1, bf16[128,256]{1,0:T(8,128)(2,1)} %nv_ref.1, bf16[1,2048,256]{2,1,0:T(8,128)(2,1)} %k_ref.1, bf16[1,2048,256]{2,1,0:T(8,128)(2,1)} %v_ref.1, bf16[128,2048]{1,0:T(8,128)(2,1)} %res_ref.1, ...), custom_call_target="tpu_custom_call" | custom-call | tf_op jit(solution)/shard_map/pallas_call | solution.py:722
  138.3 1.9 %copy.18 = bf16[128,2048]{1,0:T(8,128)(2,1)} copy(bf16[128,2048]{1,0:T(8,128)(2,1)} %shard_map.136) | data formatting | bytes 1048576
  (1 shorter events, 0.0 us)

commit v3 on v2

--- a/solution.py
+++ b/solution.py
@@ -176,40 +176,40 @@
 XWAY = 4
 TILE = 16
 P0, P1, PR, Q0, Q1, QS = range(6)
-A_SLOTS = 6
-SHARE_ROWS = 32
-
-
-def gather_events(*items):
-    codes = [kind * 4 + nb for kind, nb in items]
-    codes += [31] * (A_SLOTS - len(codes))
-    return sum(c << (5 * j) for j, c in enumerate(codes))
-
-
+A_UP, A_DOWN, A_PASS, ATTEND, PROJECT = range(6, 11)
+A_KINDS = {"P0": P0, "P1": P1, "PR": PR, "Q0": Q0, "Q1": Q1, "QS": QS}
+A_OWN = {"u": A_UP, "d": A_DOWN, "y": A_PASS}
 A_END = (
-    gather_events(), gather_events(), gather_events(),
-    gather_events((Q0, 0), (P0, 1)),
-    gather_events((Q1, 0)),
-    gather_events((P1, 1)),
-    gather_events((QS, 0), (Q0, 1)),
-    gather_events((P0, 2), (PR, 1), (Q1, 1)),
-    gather_events((P1, 2), (QS, 1)),
-    gather_events((Q0, 2), (PR, 2), (P0, 3)),
-    gather_events((Q1, 2), (QS, 2)),
-    gather_events((P1, 3), (Q0, 3), (PR, 3), (Q1, 3), (QS, 3)),
+    "yQ0", "uP0", "a", "uP1", "a", "0Q0", "1P0", "a", "yQ1", "a", "a", "1Q0",
+    "1P1", "a", "a", "2P0", "a", "1QS", "0Q1", "3P0", "0QS", "j01", "1Q1", "j10",
+    "2Q0", "1PR", "3PR", "3P1", "2PR", "j00", "3Q0", "2P1", "2QS", "j21", "j31", "j11",
+    "2Q1", "3Q1", "3QS", "j20", "j30",
 )
 A_INNER = (
-    gather_events(), gather_events(), gather_events(),
-    gather_events((Q0, 1), (P0, 0), (P0, 2)),
-    gather_events((Q1, 1)),
-    gather_events((P1, 0), (P1, 2)),
-    gather_events((QS, 1), (Q0, 0)),
-    gather_events((P0, 3), (PR, 0), (PR, 2)),
-    gather_events((Q0, 2), (P1, 3)),
-    gather_events((Q1, 0), (QS, 0)),
-    gather_events((Q1, 2), (QS, 2)),
-    gather_events((Q0, 3), (PR, 3), (Q1, 3), (QS, 3)),
+    "yQ0", "yQ1", "dP0", "uP0", "dP1", "a", "a", "1Q0", "0P0", "a", "2P0", "0P1",
+    "3P0", "a", "1QS", "uP1", "a", "3P1", "0Q0", "a", "a", "2P1", "a", "2Q0",
+    "2PR", "j21", "0PR", "3PR", "j11", "3Q0", "0Q1", "1Q1", "j01", "0QS", "j10", "j00",
+    "j31", "2Q1", "3Q1", "2QS", "3QS", "j20", "j30",
 )
+
+
+def gather_code(text):
+    if text == "a":
+        return ATTEND * 8
+    if text[0] in A_OWN:
+        return A_OWN[text[0]] * 8 + int(text[2])
+    if text[0] == "j":
+        return PROJECT * 8 + int(text[1]) * 2 + int(text[2])
+    return A_KINDS[text[1:]] * 8 + int(text[0]) * 2
+
+
+def packed(codes, words, bits):
+    codes = codes + [(1 << bits) - 1] * (words * (28 // bits) - len(codes))
+    per = 28 // bits
+    return [
+        sum(c << (bits * j) for j, c in enumerate(codes[per * w : per * w + per]))
+        for w in range(words)
+    ]
 
 
 def pick(index, inner, ends, inners):
@@ -225,37 +225,36 @@
 KINDS = {"g": GET, "u": UP_OWN, "d": DOWN_OWN, "y": PASS_OWN}
 KINDS.update({"s": SERVE, "p": PAIR_UP, "f": FOLD, "z": FINISH})
 PA, PB, PC, PD = range(4)
+SUBS = 2
 B_END = (
-    "uc", "ua", "ya", "yc", "g0b", "ub", "g1b", "g1a", "s11", "g3c", "g0d", "s00",
-    "g3d", "g3a", "f11", "s30", "f12", "g3b", "p0", "p3", "s31", "f32", "f31", "s01",
-    "g2c", "g2a", "f30", "g2b", "s21", "g2d", "g1c", "f22", "s20", "f21", "g1d", "p2",
-    "s10", "p1", "f20", "z2", "f10", "z0", "z1",
+    "ya1", "uc0", "uc1", "ya0", "g0b1", "yc1", "ua1", "g0b0", "ub1", "ua0", "s01", "g1b0",
+    "yc0", "g0d1", "g1b1", "g1a0", "g1a1", "ub0", "g3c0", "g3c1", "s11", "g3d1", "g3d0", "f12",
+    "s30", "g3a1", "g0d0", "p3", "f11", "s00", "g3a0", "g3b1", "g3b0", "g2c1", "p0", "f30",
+    "s31", "g2b1", "f32", "g2a1", "g2b0", "g2a0", "g2d1", "f31", "g2c0", "s21", "g1c1", "g2d0",
+    "f22", "g1c0", "s20", "g1d1", "f21", "g1d0", "p2", "s10", "p1", "f20", "z2", "z0",
+    "f10", "z1",
 )
 B_INNER = (
-    "ya", "uc", "da", "g0c", "g1b", "db", "g0a", "yc", "g3c", "g0b", "g3a", "s11",
-    "ua", "g0d", "g3b", "g2c", "g1d", "s31", "ub", "g2a", "g3d", "s30", "s00", "g2b",
-    "p3", "dc", "s10", "p0", "f32", "s21", "f31", "p1", "s01", "g2d", "f30", "f02",
-    "s20", "f22", "p2", "f01", "f21", "f00", "z2", "f20", "z1", "z0",
+    "da1", "ya1", "uc1", "ya0", "da0", "ua0", "g0c0", "g1b1", "db1", "g1b0", "db0", "yc1",
+    "g0c1", "g0a1", "yc0", "g3c0", "g3c1", "g2a0", "g0b1", "g0d0", "s11", "g2c1", "g0a0", "g0b0",
+    "g0d1", "ub1", "g3a1", "ua1", "s00", "uc0", "g3d0", "g3d1", "g3a0", "g1d0", "g3b1", "s30",
+    "g3b0", "p3", "g2d1", "g2b1", "g2a1", "ub0", "g1d1", "s31", "g2b0", "p0", "s01", "g2c0",
+    "dc1", "f30", "s21", "g2d0", "dc0", "f32", "s20", "f00", "f31", "s10", "p2", "f22",
+    "p1", "f02", "f21", "f01", "z2", "f20", "z1", "z0",
 )
 
 
 def code_of(text):
-    kind = KINDS[text[0]]
-    if kind == GET:
-        return kind * 16 + int(text[1]) * 4 + PIECES.index(text[2])
-    if kind in (UP_OWN, DOWN_OWN, PASS_OWN):
-        return kind * 16 + PIECES.index(text[1])
-    if kind == PAIR_UP:
-        return kind * 16 + int(text[1]) * 4
-    if kind == FINISH:
-        return kind * 16 + int(text[1])
-    return kind * 16 + int(text[1]) * 4 + int(text[2])
-
-
-def packed(program, words):
-    codes = [code_of(text) for text in program]
-    codes += [127] * (4 * words - len(codes))
-    return [sum(c << (7 * j) for j, c in enumerate(codes[4 * w : 4 * w + 4])) for w in range(words)]
+    kind = KINDS[text[0]] * 32
+    if kind == GET * 32:
+        return kind + int(text[1]) * 8 + PIECES.index(text[2]) * 2 + int(text[3])
+    if kind in (UP_OWN * 32, DOWN_OWN * 32, PASS_OWN * 32):
+        return kind + PIECES.index(text[1]) * 2 + int(text[2])
+    if kind == PAIR_UP * 32:
+        return kind + int(text[1]) * 8
+    if kind == FINISH * 32:
+        return kind + int(text[1]) * 2
+    return kind + int(text[1]) * 8 + int(text[2]) * 2
 
 
 def first_serve(program):
@@ -263,8 +262,8 @@
 
 
 def layer_kernel(
-    length_ref, q_ref, nk_ref, nv_ref, k_ref, v_ref, res_ref, gain_ref, share_ref, ow_ref,
-    wg_ref, wu_ref, wd_ref, out_ref,
+    length_ref, nk_ref, nv_ref, res_ref, gain_ref, ids_ref, raw_ref, q_hbm, k_hbm, v_hbm, ow_ref,
+    wg_ref, wu_ref, wd_ref, out_ref, q_ref, k_ref, v_ref,
     held, attn, mixed_ref, share_tab, share_col, rows, part, from_twin, from_pair, from_line, acc,
     wg, wu, wd, own_sem, load_sem, send_sem, recv_sem, share_send, share_recv,
     row_send, row_recv, back_send, twin_sem, pair_sem, line_sem,
@@ -279,13 +278,14 @@
     step_up = jnp.where(low, 1, -1)
     own = pltpu.make_async_copy(ow_ref, held.at[place.me], own_sem)
     own.start()
-    loads = [
+    pairs = ((q_hbm, q_ref), (k_hbm, k_ref), (v_hbm, v_ref), (wg_ref, wg), (wu_ref, wu), (wd_ref, wd))
+    fetches = [
         pltpu.make_async_copy(source, dest, load_sem.at[k])
-        for k, (source, dest) in enumerate(((wg_ref, wg), (wu_ref, wu), (wd_ref, wd)))
+        for k, (source, dest) in enumerate(pairs)
     ]
-    for load in loads:
-        load.start()
-    share_tab[place.me] = share_ref[...]
+    fetches, loads = fetches[:3], fetches[3:]
+    for fetch in fetches:
+        fetch.start()
     place.barrier(True)
     own.wait()
 
@@ -343,21 +343,52 @@
         return place.block(real(nb), yb, c)
 
     me = place.me
-    copy(me, P0, UPN).start()
-    pl.when(inner == 1)(copy(me, P0, DOWNN).start)
-    copy(me, Q0, ACROSS).start()
-    copy(me, P1, UPN).start()
-    pl.when(inner == 1)(copy(me, P1, DOWNN).start)
-    copy(me, Q1, ACROSS).start()
     whole(me).start()
-    share_copy(me, UPN).start()
-    pl.when(inner == 1)(share_copy(me, DOWNN).start)
-    share_copy(me, ACROSS).start()
-    share_copy(me, TWIN).start()
-
-    def happen(code):
-        nb = lax.rem(code, 4)
-        kind = code // 4
+
+    def share_out():
+        raw = raw_ref[...]
+        given_share = raw / jnp.sum(raw, axis=0, keepdims=True)
+        expert = lax.broadcasted_iota(jnp.int32, (share_tab.shape[1], 1), 0)
+        table = jnp.zeros(share_tab.shape[1:], jnp.float32)
+        for k in range(TOPK):
+            hit = ids_ref[k : k + 1] == expert
+            table = table + jnp.where(hit, given_share[k : k + 1], 0.0)
+        share_tab[me] = table
+        share_copy(me, UPN).start()
+        pl.when(inner == 1)(share_copy(me, DOWNN).start)
+        share_copy(me, ACROSS).start()
+        share_copy(me, TWIN).start()
+
+    def happen(code, turn):
+        nb = lax.rem(code // 2, 4)
+        flag = lax.rem(code, 2)
+        kind = code // 8
+
+        def own_line(way):
+            pl.when(flag == 0)(copy(me, P0, way).start)
+            pl.when(flag == 1)(copy(me, P1, way).start)
+
+        pl.when(kind == A_UP)(lambda: own_line(UPN))
+        pl.when(kind == A_DOWN)(lambda: own_line(DOWNN))
+
+        @pl.when(kind == A_PASS)
+        def _():
+            pl.when(flag == 0)(copy(me, Q0, ACROSS).start)
+            pl.when(flag == 1)(copy(me, Q1, ACROSS).start)
+
+        @pl.when(kind == ATTEND)
+        def _():
+            @pl.when(turn == 0)
+            def _():
+                share_out()
+                for load in loads:
+                    load.start()
+                for fetch in fetches:
+                    fetch.wait()
+
+            attend_step(turn)
+
+        pl.when(kind == PROJECT)(lambda: project(nb, flag == 1))
         own_b = block_at(nb, y, core)
         other_b = block_at(nb, 1 - y, core)
 
@@ -409,7 +440,6 @@
             copy(other_b, QS, TWIN).start()
 
     length = length_ref[place.me]
-    attends = HEADS // PACK
     per_group = HEADS // KV_HEADS // PACK
 
     def attend_step(i):
@@ -431,8 +461,7 @@
             ]
 
     mixed_ref[...] = res_ref[...].astype(jnp.float32)
-    lane = lax.broadcasted_iota(jnp.int32, (1, SHARE_ROWS), 1)
-    chosen = (lane == me) | (lane == me + SHARE_ROWS // 2)
+    chosen = lax.broadcasted_iota(jnp.int32, (1, share_tab.shape[1]), 1) == me
 
     def project(nb, is_own):
         yb = jnp.where(is_own, y, 1 - y)
@@ -455,35 +484,27 @@
         share_copy(b, TWIN).wait_recv()
         first = block_at(nb, yb, 0)
         for c in range(2):
-            turned = share_tab[first + c].astype(jnp.float32).T
+            turned = share_tab[first + c].T
             column = jnp.sum(jnp.where(chosen, turned, 0.0), axis=1, keepdims=True)
             share_col[first + c] = jnp.broadcast_to(column, share_col.shape[1:])
         mine = attn[:, pl.ds(pl.multiple_of(first * depth, 2 * depth), 2 * depth)]
         weight = held[pl.ds(first, 2)].reshape(2 * depth, D)
         mixed_ref[...] += jnp.dot(mine, weight, preferred_element_type=jnp.float32)
 
-    def step(s, carry):
-        def one(j, word):
-            code = lax.rem(word, 32)
-            pl.when(code < 31)(lambda: happen(code))
-            return word // 32
-
-        lax.fori_loop(0, A_SLOTS, one, pick(s, inner, A_END, A_INNER))
-        pl.when(s < attends)(lambda: attend_step(s))
-
-        @pl.when(s >= attends)
-        def _():
-            nb = pick(s - attends, inner, (0, 1, 2, 3), (1, 0, 2, 3))
-
-            def both(k, inside):
-                project(nb, k == 0)
-                return inside
-
-            lax.fori_loop(0, 2, both, 0)
-
-        return carry
-
-    lax.fori_loop(0, len(A_END), step, 0)
+    a_words = -(-max(len(A_END), len(A_INNER)) // 4)
+    a_end = packed([gather_code(text) for text in A_END], a_words, 7)
+    a_inner = packed([gather_code(text) for text in A_INNER], a_words, 7)
+
+    def gather_route(w, turn):
+        def one(j, state):
+            word, at = state
+            code = lax.rem(word, 128)
+            happen(code, at)
+            return word // 128, at + jnp.where(code // 8 == ATTEND, 1, 0)
+
+        return lax.fori_loop(0, 4, one, (pick(w, inner, a_end, a_inner), turn))[1]
+
+    lax.fori_loop(0, a_words, gather_route, jnp.int32(0))
     half_rows = tokens // 2
     mixed = mixed_ref[...]
     scale = lax.rsqrt(jnp.mean(mixed * mixed, axis=-1, keepdims=True) + 1e-06)
@@ -492,8 +513,11 @@
     def slot(zb, p, yb, c):
         return ((zb * 2 + p) * PAIR + yb) * 2 + c
 
+    sub = half_rows // SUBS
     for p in range(2):
-        rows[slot(z, p, y, core)] = normed[p * half_rows : (p + 1) * half_rows]
+        for h in range(SUBS):
+            first_row = p * half_rows + h * sub
+            rows[slot(z, p, y, core) * SUBS + h] = normed[first_row : first_row + sub]
 
     def send(source, dest, send_one, recv_one, way):
         return pltpu.make_async_remote_copy(
@@ -501,8 +525,9 @@
             device_id=device(way), device_id_type=pl.DeviceIdType.MESH,
         )
 
-    def row_copy(b, way):
-        return send(rows.at[b], rows.at[b], row_send.at[b, way], row_recv.at[b], way)
+    def row_copy(b, h, way):
+        t = b * SUBS + h
+        return send(rows.at[t], rows.at[t], row_send.at[t, way], row_recv.at[t], way)
 
     def to_twin(zb, p, yb):
         b = slot(zb, p, yb, 1 - core)
@@ -531,9 +556,10 @@
 
     def serve(zb, p):
         for yb in range(2):
-            row_copy(slot(zb, p, yb, 1 - core), TWIN).wait_recv()
+            for h in range(SUBS):
+                row_copy(slot(zb, p, yb, 1 - core), h, TWIN).wait_recv()
         first = slot(zb, p, 0, 0)
-        x = rows[pl.ds(first, 4)].reshape(4 * half_rows, D)
+        x = rows[pl.ds(first * SUBS, 4 * SUBS)].reshape(4 * half_rows, D)
         here = pl.ds(pl.multiple_of(p * half_rows, half_rows), half_rows)
         share = share_col[pl.ds(place.block(zb, 0, 0), 4), here].reshape(4 * half_rows, HEAD)
         gate = jnp.dot(x, wg[...], preferred_element_type=jnp.float32)
@@ -593,9 +619,10 @@
         pl.when(kind == 1)(lambda: close(1, LINE))
 
     def act_on(code, first):
-        kind = code // 16
-        nb = lax.rem(code // 4, 4)
-        piece = lax.rem(code, 4)
+        kind = code // 32
+        nb = lax.rem(code // 8, 4)
+        piece = lax.rem(code // 2, 4)
+        h = lax.rem(code, 2)
         zb = real(nb)
         p = jnp.where(piece <= PB, 1, 0)
         yb = jnp.where((piece == PA) | (piece == PC), y, 1 - y)
@@ -604,20 +631,20 @@
         @pl.when(kind == GET)
         def _():
             b = slot(zb, p, yb, core)
-            row_copy(b, TWIN).wait_recv()
+            row_copy(b, h, TWIN).wait_recv()
             onward = piece != PD
-            pl.when(onward & (nb < inner))(row_copy(b, UPN).start)
-            pl.when(onward & (nb > inner) & (inner == 1))(row_copy(b, DOWNN).start)
-            pl.when((piece == PC) & (nb != inner))(row_copy(b, ACROSS).start)
-            row_copy(b, TWIN).start()
-
-        pl.when(kind == UP_OWN)(row_copy(own_piece, UPN).start)
-        pl.when(kind == DOWN_OWN)(row_copy(own_piece, DOWNN).start)
+            pl.when(onward & (nb < inner))(row_copy(b, h, UPN).start)
+            pl.when(onward & (nb > inner) & (inner == 1))(row_copy(b, h, DOWNN).start)
+            pl.when((piece == PC) & (nb != inner))(row_copy(b, h, ACROSS).start)
+            row_copy(b, h, TWIN).start()
+
+        pl.when(kind == UP_OWN)(row_copy(own_piece, h, UPN).start)
+        pl.when(kind == DOWN_OWN)(row_copy(own_piece, h, DOWNN).start)
 
         @pl.when(kind == PASS_OWN)
         def _():
-            row_copy(own_piece, ACROSS).start()
-            row_copy(own_piece, TWIN).start()
+            row_copy(own_piece, h, ACROSS).start()
+            row_copy(own_piece, h, TWIN).start()
 
         @pl.when(kind == SERVE)
         def _():
@@ -636,31 +663,35 @@
         pl.when(kind == FOLD)(lambda: fold(nb, piece))
         pl.when((kind == FINISH) & (piece < 3))(lambda: finish(piece))
 
-    words = -(-max(len(B_END), len(B_INNER)) // 4)
-    end_words, inner_words = packed(B_END, words), packed(B_INNER, words)
+    words = -(-max(len(B_END), len(B_INNER)) // 3)
+    end_words = packed([code_of(text) for text in B_END], words, 9)
+    inner_words = packed([code_of(text) for text in B_INNER], words, 9)
     serve_at = jnp.where(inner == 1, first_serve(B_INNER), first_serve(B_END))
 
     def route(w, carry):
         def one(j, word):
-            act_on(lax.rem(word, 128), w * 4 + j == serve_at)
-            return word // 128
-
-        lax.fori_loop(0, 4, one, pick(w, inner, end_words, inner_words))
+            act_on(lax.rem(word, 512), w * 3 + j == serve_at)
+            return word // 512
+
+        lax.fori_loop(0, 3, one, pick(w, inner, end_words, inner_words))
         return carry
 
     lax.fori_loop(0, words, route, 0)
 
     def settle_rows(nb, carry):
         zb = real(nb)
-        for p, yb in ((0, y), (1, y), (1, 1 - y)):
-            b = slot(zb, p, yb, core)
-            pl.when(nb <= inner)(row_copy(b, UPN).wait_send)
-            pl.when((nb >= inner) & (inner == 1))(row_copy(b, DOWNN).wait_send)
-        row_copy(slot(zb, 0, y, core), ACROSS).wait_send()
-        pl.when(nb == inner)(row_copy(slot(zb, 1, y, core), ACROSS).wait_send)
+        for h in range(SUBS):
+            for p, yb in ((0, y), (1, y), (1, 1 - y)):
+                b = slot(zb, p, yb, core)
+                pl.when(nb <= inner)(row_copy(b, h, UPN).wait_send)
+                pl.when((nb >= inner) & (inner == 1))(row_copy(b, h, DOWNN).wait_send)
+            row_copy(slot(zb, 0, y, core), h, ACROSS).wait_send()
+            pl.when(nb == inner)(row_copy(slot(zb, 1, y, core), h, ACROSS).wait_send)
+            for p in range(2):
+                for yb in (y, 1 - y):
+                    row_copy(slot(zb, p, yb, core), h, TWIN).wait_send()
         for p in range(2):
             for yb in (y, 1 - y):
-                row_copy(slot(zb, p, yb, core), TWIN).wait_send()
                 to_twin(zb, p, yb).wait_send()
         to_pair(zb, 0).wait_send()
         pl.when(nb == inner)(to_pair(zb, 1).wait_send)
@@ -707,7 +738,7 @@
 
 
 def layer(
-    cache_len, queries, new_keys, new_values, cache_keys, cache_values, residual, gain, shares,
+    cache_len, queries, new_keys, new_values, cache_keys, cache_values, residual, gain, ids, raw,
     o_weight, gate_w, up_w, down_w, devices,
 ):
     tokens, width = queries.shape
@@ -721,16 +752,19 @@
 
     return pl.pallas_call(
         layer_kernel,
-        in_specs=[pl.BlockSpec(memory_space=pltpu.SMEM)] + [vmem] * 8 + [whole] * 4,
+        in_specs=[pl.BlockSpec(memory_space=pltpu.SMEM)] + [vmem] * 6 + [whole] * 7,
         out_specs=vmem,
         out_shape=jax.ShapeDtypeStruct((tokens, D), jnp.bfloat16),
         scratch_shapes=[
+            pltpu.VMEM(queries.shape, jnp.bfloat16),
+            pltpu.VMEM(cache_keys.shape, jnp.bfloat16),
+            pltpu.VMEM(cache_values.shape, jnp.bfloat16),
             pltpu.VMEM((devices,) + o_weight.shape, jnp.bfloat16),
             pltpu.VMEM((tokens, width), jnp.bfloat16),
             pltpu.VMEM((tokens, D), jnp.float32),
-            pltpu.VMEM((devices,) + shares.shape, jnp.bfloat16),
+            pltpu.VMEM((devices, devices, tokens), jnp.float32),
             pltpu.VMEM((devices, tokens, HEAD), jnp.float32),
-            held(2 * devices),
+            pltpu.VMEM((2 * devices * SUBS, half // SUBS, D), jnp.bfloat16),
             held(2 * devices),
             held(devices),
             held(LINE + 1),
@@ -740,13 +774,13 @@
             pltpu.VMEM(up_w.shape, jnp.bfloat16),
             pltpu.VMEM(down_w.shape, jnp.bfloat16),
             dma,
-            dma((3,)),
+            dma((6,)),
             dma((devices, 3, 5)),
             dma((devices, 3)),
             dma((devices, 4)),
             dma((devices,)),
-            dma((2 * devices, 4)),
-            dma((2 * devices,)),
+            dma((2 * devices * SUBS, 4)),
+            dma((2 * devices * SUBS,)),
             dma((2 * devices,)),
             dma((devices,)),
             dma((LINE + 1,)),
@@ -756,7 +790,7 @@
             collective_id=0, has_side_effects=True, vmem_limit_bytes=63 << 20
         ),
     )(
-        cache_len, queries, new_keys, new_values, cache_keys, cache_values, residual, gain, shares,
+        cache_len, new_keys, new_values, residual, gain, ids, raw, queries, cache_keys, cache_values,
         o_weight, gate_w, up_w, down_w,
     )
 
@@ -766,15 +800,9 @@
     norm_gain, expert_ids, gate_raw, w_gate, w_up, w_down,
 ):
     devices = lax.axis_size("wide")
-    parts = gate_raw / jnp.sum(gate_raw, axis=-1, keepdims=True)
-    hits = expert_ids[:, :, None] == jnp.arange(devices, dtype=jnp.int32)[None, None, :]
-    share_of = jnp.sum(jnp.where(hits, parts[..., None], 0.0), axis=1)
-    coarse = share_of.astype(jnp.bfloat16)
-    fine = (share_of - coarse.astype(jnp.float32)).astype(jnp.bfloat16)
-    shares = jnp.concatenate([coarse, fine], axis=1).T
     return layer(
         cache_len, queries, new_keys, new_values, cache_keys, cache_values, residual,
-        norm_gain.reshape(1, D), shares, o_weight, w_gate[0], w_up[0], w_down[0], devices,
+        norm_gain.reshape(1, D), expert_ids.T, gate_raw.T, o_weight, w_gate[0], w_up[0], w_down[0], devices,
     )
 
 

time: 141 us -> 131 us (0.929)
  Pallas kernels: 136 us -> 128 us
  other arithmetic: 2.7 us -> 0 us
    pallas_call x1, Pallas kernels: 136 us -> 128 us  [layer(): pl.pallas_call(layer_kernel, in_specs=[pl.BlockSpec(memory_space=pltpu.SM...]
where the time goes in v3:
time: 131 us; the launch traced here: 130 us
  Pallas kernels  128 us (98%)
  local copies, waits for them, and re-layouts  1.88 us (1%)
    pallas_call x1, Pallas kernels, layer(): pl.pallas_call(layer_kernel, in_specs=[pl.BlockSpec(memory_space=pltpu.SM...  128 us

profile of v3, /device:TPU:0, one launch (start us, length us, event | category | flops | bytes accessed | tf_op | source)
XLA Modules:
  0.0 129.5 jit_solution(764699360175088213)
XLA Ops:
  0.0 127.6 %shard_map.136 = bf16[128,2048]{1,0:T(8,128)(2,1)} custom-call(s32[16]{0:T(128)} %length_ref.1, bf16[128,256]{1,0:T(8,128)(2,1)} %nk_ref.1, bf16[128,256]{1,0:T(8,128)(2,1)} %nv_ref.1, bf16[128,2048]{1,0:T(8,128)(2,1)} %res_ref.1, f32[1,2048]{1,0:T(1,128)} %bitcast.9, s32[8,128]{1,0:T(8,128)} %bitcast.10, f32[8,128]{1,0:T(8,128)} %bitcast.11, ...), custom_call_target="tpu_custom_call" | custom-call | tf_op jit(solution)/shard_map/pallas_call | solution.py:753
  127.6 1.9 %copy.16 = bf16[128,2048]{1,0:T(8,128)(2,1)} copy(bf16[128,2048]{1,0:T(8,128)(2,1)} %shard_map.136) | data formatting | bytes 1048576

commit v4 on v3

--- a/solution.py
+++ b/solution.py
@@ -265,8 +265,8 @@
     length_ref, nk_ref, nv_ref, res_ref, gain_ref, ids_ref, raw_ref, q_hbm, k_hbm, v_hbm, ow_ref,
     wg_ref, wu_ref, wd_ref, out_ref, q_ref, k_ref, v_ref,
     held, attn, mixed_ref, share_tab, share_col, rows, part, from_twin, from_pair, from_line, acc,
-    wg, wu, wd, own_sem, load_sem, send_sem, recv_sem, share_send, share_recv,
-    row_send, row_recv, back_send, twin_sem, pair_sem, line_sem,
+    wg, wu, wd, own_sem, load_sem, send_sem, recv_sem, recv_twin, share_send,
+    share_recv, row_send, row_recv, twin_rows, back_send, twin_sem, pair_sem, line_sem,
 ):
     place = Place()
     z, y, core = place.z, place.y, place.core
@@ -319,22 +319,25 @@
         if not isinstance(start, int):
             start = pl.multiple_of(start, TILE)
         ref = held.at[b, pl.ds(start, size)]
-        i = what % 3
         return pltpu.make_async_remote_copy(
-            src_ref=ref, dst_ref=ref, send_sem=send_sem.at[b, i, way], recv_sem=recv_sem.at[b, i],
+            src_ref=ref, dst_ref=ref, send_sem=send_sem.at[way],
+            recv_sem=recv_twin.at[b // 2] if way == TWIN else recv_sem.at[b // 2, what % 3],
             device_id=device(way), device_id_type=pl.DeviceIdType.MESH,
         )
 
+    def arrived(b, what):
+        copy(b, what, ACROSS).wait_recv()
+
     def whole(b):
         return pltpu.make_async_remote_copy(
-            src_ref=held.at[b], dst_ref=held.at[b], send_sem=send_sem.at[b, 2, TWIN],
-            recv_sem=recv_sem.at[b, 0], device_id=device(TWIN),
+            src_ref=held.at[b], dst_ref=held.at[b], send_sem=send_sem.at[TWIN],
+            recv_sem=recv_twin.at[b // 2], device_id=device(TWIN),
             device_id_type=pl.DeviceIdType.MESH,
         )
 
     def share_copy(b, way):
         return pltpu.make_async_remote_copy(
-            src_ref=share_tab.at[b], dst_ref=share_tab.at[b], send_sem=share_send.at[b, way],
+            src_ref=share_tab.at[b], dst_ref=share_tab.at[b], send_sem=share_send.at[way],
             recv_sem=share_recv.at[b], device_id=device(way),
             device_id_type=pl.DeviceIdType.MESH,
         )
@@ -398,7 +401,7 @@
 
         @pl.when(kind == P0)
         def _():
-            copy(own_b, P0, TWIN).wait_recv()
+            arrived(own_b, P0)
             line(P0)
             copy(own_b, Q0, ACROSS).start()
             copy(own_b, PR, XWAY).start()
@@ -411,19 +414,19 @@
 
         @pl.when(kind == P1)
         def _():
-            copy(own_b, P1, TWIN).wait_recv()
+            arrived(own_b, P1)
             line(P1)
             copy(own_b, Q1, ACROSS).start()
             copy(own_b, P1, TWIN).start()
 
         @pl.when(kind == PR)
         def _():
-            copy(own_b, PR, TWIN).wait_recv()
+            arrived(own_b, PR)
             copy(own_b, PR, TWIN).start()
 
         @pl.when(kind == Q0)
         def _():
-            copy(other_b, Q0, TWIN).wait_recv()
+            arrived(other_b, Q0)
             copy(other_b, QS, XWAY).start()
             copy(other_b, Q0, TWIN).start()
             share_copy(other_b, TWIN).wait_recv()
@@ -431,12 +434,12 @@
 
         @pl.when(kind == Q1)
         def _():
-            copy(other_b, Q1, TWIN).wait_recv()
+            arrived(other_b, Q1)
             copy(other_b, Q1, TWIN).start()
 
         @pl.when(kind == QS)
         def _():
-            copy(other_b, QS, TWIN).wait_recv()
+            arrived(other_b, QS)
             copy(other_b, QS, TWIN).start()
 
     length = length_ref[place.me]
@@ -467,20 +470,7 @@
         yb = jnp.where(is_own, y, 1 - y)
         b = block_at(nb, yb, 1 - core)
 
-        @pl.when(is_own & (nb == inner))
-        def _():
-            whole(b).wait_recv()
-
-        @pl.when(is_own & (nb != inner))
-        def _():
-            for what in (P0, P1, PR):
-                copy(b, what, TWIN).wait_recv()
-
-        @pl.when(jnp.logical_not(is_own))
-        def _():
-            for what in (Q0, Q1, QS):
-                copy(b, what, TWIN).wait_recv()
-
+        whole(b).wait_recv()
         share_copy(b, TWIN).wait_recv()
         first = block_at(nb, yb, 0)
         for c in range(2):
@@ -527,17 +517,18 @@
 
     def row_copy(b, h, way):
         t = b * SUBS + h
-        return send(rows.at[t], rows.at[t], row_send.at[t, way], row_recv.at[t], way)
+        landed = twin_rows.at[b // 4] if way == TWIN else row_recv.at[b // 2 * SUBS + h]
+        return send(rows.at[t], rows.at[t], row_send.at[way], landed, way)
 
     def to_twin(zb, p, yb):
         b = slot(zb, p, yb, 1 - core)
         t = (zb * 2 + p) * PAIR + yb
-        return send(part.at[b], from_twin.at[t], back_send.at[b], twin_sem.at[t], TWIN)
+        return send(part.at[b], from_twin.at[t], back_send.at[0], twin_sem.at[t], TWIN)
 
     def to_pair(zb, p):
         b = slot(zb, p, 1 - y, core)
         t = LINE if p else zb
-        return send(part.at[b], from_pair.at[t], back_send.at[b], pair_sem.at[t], ACROSS)
+        return send(part.at[b], from_pair.at[t], back_send.at[0], pair_sem.at[t], ACROSS)
 
     def kind_slot(zb, kind):
         p = jnp.minimum(kind, 1)
@@ -550,15 +541,14 @@
         b = kind_slot(zb, kind)[2]
         side = side_up if way == UPN else 1 - side_up
         return send(
-            part.at[b], from_line.at[side, zb, kind], back_send.at[b],
+            part.at[b], from_line.at[side, zb, kind], back_send.at[0],
             line_sem.at[side, zb, kind], way,
         )
 
     def serve(zb, p):
-        for yb in range(2):
-            for h in range(SUBS):
-                row_copy(slot(zb, p, yb, 1 - core), h, TWIN).wait_recv()
         first = slot(zb, p, 0, 0)
+        bulk = rows.at[pl.ds(0, 2 * SUBS)]
+        send(bulk, bulk, row_send.at[TWIN], twin_rows.at[first // 4], TWIN).wait_recv()
         x = rows[pl.ds(first * SUBS, 4 * SUBS)].reshape(4 * half_rows, D)
         here = pl.ds(pl.multiple_of(p * half_rows, half_rows), half_rows)
         share = share_col[pl.ds(place.block(zb, 0, 0), 4), here].reshape(4 * half_rows, HEAD)
@@ -631,7 +621,7 @@
         @pl.when(kind == GET)
         def _():
             b = slot(zb, p, yb, core)
-            row_copy(b, h, TWIN).wait_recv()
+            row_copy(b, h, ACROSS).wait_recv()
             onward = piece != PD
             pl.when(onward & (nb < inner))(row_copy(b, h, UPN).start)
             pl.when(onward & (nb > inner) & (inner == 1))(row_copy(b, h, DOWNN).start)
@@ -678,63 +668,41 @@
 
     lax.fori_loop(0, words, route, 0)
 
-    def settle_rows(nb, carry):
-        zb = real(nb)
-        for h in range(SUBS):
-            for p, yb in ((0, y), (1, y), (1, 1 - y)):
-                b = slot(zb, p, yb, core)
-                pl.when(nb <= inner)(row_copy(b, h, UPN).wait_send)
-                pl.when((nb >= inner) & (inner == 1))(row_copy(b, h, DOWNN).wait_send)
-            row_copy(slot(zb, 0, y, core), h, ACROSS).wait_send()
-            pl.when(nb == inner)(row_copy(slot(zb, 1, y, core), h, ACROSS).wait_send)
-            for p in range(2):
-                for yb in (y, 1 - y):
-                    row_copy(slot(zb, p, yb, core), h, TWIN).wait_send()
-        for p in range(2):
-            for yb in (y, 1 - y):
-                to_twin(zb, p, yb).wait_send()
-        to_pair(zb, 0).wait_send()
-        pl.when(nb == inner)(to_pair(zb, 1).wait_send)
-
-        @pl.when(nb != inner)
-        def _():
-            for kind in range(3):
-                to_line(zb, kind, UPN).wait_send()
-
-        return carry
-
-    lax.fori_loop(0, LINE, settle_rows, 0)
-
-    def settle_weights(nb, carry):
-        own_b = block_at(nb, y, core)
-        other_b = block_at(nb, 1 - y, core)
-        for what in (P0, P1):
-            pl.when(nb <= inner)(copy(own_b, what, UPN).wait_send)
-            pl.when((nb >= inner) & (inner == 1))(copy(own_b, what, DOWNN).wait_send)
-        pl.when(nb <= inner)(share_copy(own_b, UPN).wait_send)
-        pl.when((nb >= inner) & (inner == 1))(share_copy(own_b, DOWNN).wait_send)
-        share_copy(own_b, ACROSS).wait_send()
-        share_copy(own_b, TWIN).wait_send()
-        share_copy(other_b, TWIN).wait_send()
-        copy(own_b, Q0, ACROSS).wait_send()
-        copy(own_b, Q1, ACROSS).wait_send()
-
-        @pl.when(nb == inner)
-        def _():
-            whole(own_b).wait_send()
-
-        @pl.when(nb != inner)
-        def _():
-            copy(own_b, PR, XWAY).wait_send()
-            for what in (P0, P1, PR):
-                copy(own_b, what, TWIN).wait_send()
-
-        copy(other_b, QS, XWAY).wait_send()
-        for what in (Q0, Q1, QS):
-            copy(other_b, what, TWIN).wait_send()
-        return carry
-
-    lax.fori_loop(0, LINE, settle_weights, 0)
+    def sent(ref, sem, way=TWIN):
+        send(ref, ref, sem, share_recv.at[0], way).wait_send()
+
+    def sent_by_place(at_end, at_inner):
+        pl.when(inner == 0)(at_end)
+        pl.when(inner == 1)(at_inner)
+
+    lines = 2 * half
+    sent_by_place(
+        lambda: sent(held.at[0, pl.ds(0, lines)], send_sem.at[UPN]),
+        lambda: sent(held.at[pl.ds(0, 2), pl.ds(0, lines)], send_sem.at[UPN]),
+    )
+    sent_by_place(
+        lambda: sent(share_tab.at[pl.ds(0, 1)], share_send.at[UPN]),
+        lambda: sent(share_tab.at[pl.ds(0, 2)], share_send.at[UPN]),
+    )
+    sent_by_place(
+        lambda: sent(rows.at[pl.ds(0, 3 * SUBS)], row_send.at[UPN]),
+        lambda: sent(rows.at[pl.ds(0, 6 * SUBS)], row_send.at[UPN]),
+    )
+
+    @pl.when(inner == 1)
+    def _():
+        sent(held.at[pl.ds(0, 3), pl.ds(0, lines)], send_sem.at[DOWNN])
+        sent(share_tab.at[pl.ds(0, 3)], share_send.at[DOWNN])
+        sent(rows.at[pl.ds(0, 9 * SUBS)], row_send.at[DOWNN])
+
+    sent(held.at[pl.ds(0, LINE), pl.ds(0, depth - half)], send_sem.at[ACROSS])
+    sent(held.at[pl.ds(0, LINE - 1), pl.ds(0, lines)], send_sem.at[XWAY])
+    sent(held.at[pl.ds(0, 2 * LINE)], send_sem.at[TWIN])
+    sent(share_tab.at[pl.ds(0, LINE)], share_send.at[ACROSS])
+    sent(share_tab.at[pl.ds(0, 2 * LINE)], share_send.at[TWIN])
+    sent(rows.at[pl.ds(0, 5 * SUBS)], row_send.at[ACROSS])
+    sent(rows.at[pl.ds(0, 4 * LINE * SUBS)], row_send.at[TWIN])
+    sent(part.at[pl.ds(0, 7 * LINE + 2)], back_send.at[0])
 
 
 def layer(
@@ -775,13 +743,15 @@
             pltpu.VMEM(down_w.shape, jnp.bfloat16),
             dma,
             dma((6,)),
-            dma((devices, 3, 5)),
-            dma((devices, 3)),
-            dma((devices, 4)),
+            dma((5,)),
+            dma((devices // 2, 3)),
+            dma((devices // 2,)),
+            dma((4,)),
             dma((devices,)),
-            dma((2 * devices * SUBS, 4)),
-            dma((2 * devices * SUBS,)),
-            dma((2 * devices,)),
+            dma((4,)),
+            dma((devices * SUBS,)),
+            dma((devices // 2,)),
+            dma((1,)),
             dma((devices,)),
             dma((LINE + 1,)),
             dma((2, LINE, 3)),

time: 131 us -> 125 us (0.954)
  Pallas kernels: 128 us -> 121 us
    pallas_call x1, Pallas kernels: 128 us -> 121 us  [layer(): pl.pallas_call(layer_kernel, in_specs=[pl.BlockSpec(memory_space=pltpu.SM...]
where the time goes in v4:
time: 125 us; the launch traced here: 123 us
  Pallas kernels  121 us (97%)
  local copies, waits for them, and re-layouts  1.88 us (2%)
    pallas_call x1, Pallas kernels, layer(): pl.pallas_call(layer_kernel, in_specs=[pl.BlockSpec(memory_space=pltpu.SM...  121 us

profile of v4, /device:TPU:0, one launch (start us, length us, event | category | flops | bytes accessed | tf_op | source)
XLA Modules:
  0.0 123.3 jit_solution(11891431777090758949)
XLA Ops:
  0.0 121.5 %shard_map.136 = bf16[128,2048]{1,0:T(8,128)(2,1)} custom-call(s32[16]{0:T(128)} %length_ref.1, bf16[128,256]{1,0:T(8,128)(2,1)} %nk_ref.1, bf16[128,256]{1,0:T(8,128)(2,1)} %nv_ref.1, bf16[128,2048]{1,0:T(8,128)(2,1)} %res_ref.1, f32[1,2048]{1,0:T(1,128)} %bitcast.9, s32[8,128]{1,0:T(8,128)} %bitcast.10, f32[8,128]{1,0:T(8,128)} %bitcast.11, ...), custom_call_target="tpu_custom_call" | custom-call | tf_op jit(solution)/shard_map/pallas_call | solution.py:721
  121.5 1.9 %copy.16 = bf16[128,2048]{1,0:T(8,128)(2,1)} copy(bf16[128,2048]{1,0:T(8,128)(2,1)} %shard_map.136) | data formatting | bytes 1048576

commit v5 on v4

--- a/solution.py
+++ b/solution.py
@@ -175,29 +175,24 @@
 UPN, DOWNN = 0, 1
 XWAY = 4
 TILE = 16
-P0, P1, PR, Q0, Q1, QS = range(6)
-A_UP, A_DOWN, A_PASS, ATTEND, PROJECT = range(6, 11)
-A_KINDS = {"P0": P0, "P1": P1, "PR": PR, "Q0": Q0, "Q1": Q1, "QS": QS}
-A_OWN = {"u": A_UP, "d": A_DOWN, "y": A_PASS}
+LINE_A, LINE_B, CROSS_A, CROSS_B, A_UP, A_DOWN, ATTEND, READY, PROJECT = range(9)
+A_KINDS = {"A": LINE_A, "B": LINE_B, "XA": CROSS_A, "XB": CROSS_B}
+A_PLAIN = {"u": A_UP, "d": A_DOWN, "a": ATTEND, "r": READY}
 A_END = (
-    "yQ0", "uP0", "a", "uP1", "a", "0Q0", "1P0", "a", "yQ1", "a", "a", "1Q0",
-    "1P1", "a", "a", "2P0", "a", "1QS", "0Q1", "3P0", "0QS", "j01", "1Q1", "j10",
-    "2Q0", "1PR", "3PR", "3P1", "2PR", "j00", "3Q0", "2P1", "2QS", "j21", "j31", "j11",
-    "2Q1", "3Q1", "3QS", "j20", "j30",
+    "a", "a", "a", "0B", "u", "a", "a", "a", "1A", "1B", "a", "2A",
+    "a", "3A", "1XA", "2XA", "1XB", "0XB", "r", "2B", "j10", "j21", "j01", "3XA",
+    "2XB", "3B", "j00", "j20", "j11", "3XB", "j31", "j30",
 )
 A_INNER = (
-    "yQ0", "yQ1", "dP0", "uP0", "dP1", "a", "a", "1Q0", "0P0", "a", "2P0", "0P1",
-    "3P0", "a", "1QS", "uP1", "a", "3P1", "0Q0", "a", "a", "2P1", "a", "2Q0",
-    "2PR", "j21", "0PR", "3PR", "j11", "3Q0", "0Q1", "1Q1", "j01", "0QS", "j10", "j00",
-    "j31", "2Q1", "3Q1", "2QS", "3QS", "j20", "j30",
+    "a", "a", "2A", "0A", "1B", "u", "d", "a", "a", "3A", "0B", "a",
+    "a", "2B", "a", "3B", "a", "1XB", "0XB", "2XA", "3XA", "2XB", "0XA", "3XB",
+    "r", "j11", "j21", "j20", "j30", "j01", "j31", "j10", "j00",
 )
 
 
 def gather_code(text):
-    if text == "a":
-        return ATTEND * 8
-    if text[0] in A_OWN:
-        return A_OWN[text[0]] * 8 + int(text[2])
+    if text[0] in A_PLAIN:
+        return A_PLAIN[text[0]] * 8
     if text[0] == "j":
         return PROJECT * 8 + int(text[1]) * 2 + int(text[2])
     return A_KINDS[text[1:]] * 8 + int(text[0]) * 2
@@ -264,19 +259,23 @@
 def layer_kernel(
     length_ref, nk_ref, nv_ref, res_ref, gain_ref, ids_ref, raw_ref, q_hbm, k_hbm, v_hbm, ow_ref,
     wg_ref, wu_ref, wd_ref, out_ref, q_ref, k_ref, v_ref,
-    held, attn, mixed_ref, share_tab, share_col, rows, part, from_twin, from_pair, from_line, acc,
-    wg, wu, wd, own_sem, load_sem, send_sem, recv_sem, recv_twin, share_send,
+    held, attn, mixed_ref, res_pair, squares, share_tab, share_col, rows, part, from_twin,
+    from_pair, from_line, acc, wg, wu, wd,
+    own_sem, load_sem, send_sem, recv_sem, recv_twin, near_send, near_recv, share_send,
     share_recv, row_send, row_recv, twin_rows, back_send, twin_sem, pair_sem, line_sem,
 ):
     place = Place()
     z, y, core = place.z, place.y, place.core
     group = lax.axis_index("groups")
-    tokens = q_ref.shape[0]
-    depth = ow_ref.shape[0]
+    tokens = res_ref.shape[0]
+    depth, wide = ow_ref.shape[0], ow_ref.shape[1] // 2
     low = z < LINE // 2
     inner = jnp.where(low, z, LINE - 1 - z)
     step_up = jnp.where(low, 1, -1)
-    own = pltpu.make_async_copy(ow_ref, held.at[place.me], own_sem)
+    me = place.me
+    my_columns = pl.ds(pl.multiple_of(y * wide, wide), wide)
+    pair_columns = pl.ds(pl.multiple_of((1 - y) * wide, wide), wide)
+    own = pltpu.make_async_copy(ow_ref.at[:, my_columns], held.at[me], own_sem)
     own.start()
     pairs = ((q_hbm, q_ref), (k_hbm, k_ref), (v_hbm, v_ref), (wg_ref, wg), (wu_ref, wu), (wd_ref, wd))
     fetches = [
@@ -287,20 +286,12 @@
     for fetch in fetches:
         fetch.start()
     place.barrier(True)
-    own.wait()
-
-    third = depth // 8 * 2
-    half = depth // 8 * 3
-    last = depth - half
-    span = {
-        P0: (jnp.where(group == 0, 0, last), half),
-        P1: (jnp.where(group == 0, half, third), half),
-        PR: (jnp.where(group == 0, depth - third, 0), third),
-        Q0: (jnp.where(group == 0, 0, last), half),
-        Q1: (half, depth - 2 * half),
-        QS: (jnp.where(group == 0, last, 0), half),
-    }
-    given = {PR: (jnp.where(group == 0, 0, depth - third), third), QS: span[Q0]}
+
+    short = depth // 8 * 3
+    long = depth - short
+    line_rows = pl.ds(pl.multiple_of(jnp.where(group == 0, 0, short), TILE), long)
+    give_rows = pl.ds(pl.multiple_of(jnp.where(group == 0, 0, long), TILE), short)
+    take_rows = pl.ds(pl.multiple_of(jnp.where(group == 0, long, 0), TILE), short)
 
     def real(nb):
         return jnp.where(low, nb, LINE - 1 - nb)
@@ -314,133 +305,123 @@
             return {"wide": place.block(z - step_up, y, core)}
         return {"wide": place.towards(way)}
 
-    def copy(b, what, way):
-        start, size = given[what] if way == XWAY else span[what]
-        if not isinstance(start, int):
-            start = pl.multiple_of(start, TILE)
-        ref = held.at[b, pl.ds(start, size)]
+    def send(source, dest, send_one, recv_one, way):
         return pltpu.make_async_remote_copy(
-            src_ref=ref, dst_ref=ref, send_sem=send_sem.at[way],
-            recv_sem=recv_twin.at[b // 2] if way == TWIN else recv_sem.at[b // 2, what % 3],
+            src_ref=source, dst_ref=dest, send_sem=send_one, recv_sem=recv_one,
             device_id=device(way), device_id_type=pl.DeviceIdType.MESH,
         )
 
-    def arrived(b, what):
-        copy(b, what, ACROSS).wait_recv()
+    def copy(b, way):
+        ref = held.at[b, give_rows if way == XWAY else line_rows]
+        if way == TWIN:
+            return send(ref, ref, send_sem.at[way], recv_twin.at[b // 2], way)
+        kind = 1 if way == XWAY else 0
+        return send(ref, ref, send_sem.at[way], recv_sem.at[b // 2, kind], way)
+
+    def taken(b):
+        ref = held.at[b, take_rows]
+        return (
+            send(ref, ref, send_sem.at[XWAY], recv_sem.at[b // 2, 1], XWAY),
+            send(ref, ref, send_sem.at[TWIN], recv_twin.at[b // 2], TWIN),
+        )
 
     def whole(b):
-        return pltpu.make_async_remote_copy(
-            src_ref=held.at[b], dst_ref=held.at[b], send_sem=send_sem.at[TWIN],
-            recv_sem=recv_twin.at[b // 2], device_id=device(TWIN),
-            device_id_type=pl.DeviceIdType.MESH,
-        )
+        return send(held.at[b], held.at[b], send_sem.at[TWIN], recv_twin.at[b // 2], TWIN)
 
     def share_copy(b, way):
-        return pltpu.make_async_remote_copy(
-            src_ref=share_tab.at[b], dst_ref=share_tab.at[b], send_sem=share_send.at[way],
-            recv_sem=share_recv.at[b], device_id=device(way),
-            device_id_type=pl.DeviceIdType.MESH,
-        )
+        return send(share_tab.at[b], share_tab.at[b], share_send.at[way], share_recv.at[b], way)
 
     def block_at(nb, yb, c):
         return place.block(real(nb), yb, c)
 
-    me = place.me
+    send(
+        ow_ref.at[line_rows, pair_columns], held.at[me, line_rows], send_sem.at[ACROSS],
+        recv_sem.at[me // 2, 0], ACROSS,
+    ).start()
+    own.wait()
+    copy(me, UPN).start()
+    pl.when(inner == 1)(copy(me, DOWNN).start)
     whole(me).start()
-
-    def share_out():
-        raw = raw_ref[...]
-        given_share = raw / jnp.sum(raw, axis=0, keepdims=True)
-        expert = lax.broadcasted_iota(jnp.int32, (share_tab.shape[1], 1), 0)
-        table = jnp.zeros(share_tab.shape[1:], jnp.float32)
-        for k in range(TOPK):
-            hit = ids_ref[k : k + 1] == expert
-            table = table + jnp.where(hit, given_share[k : k + 1], 0.0)
-        share_tab[me] = table
-        share_copy(me, UPN).start()
-        pl.when(inner == 1)(share_copy(me, DOWNN).start)
-        share_copy(me, ACROSS).start()
-        share_copy(me, TWIN).start()
+    raw = raw_ref[...]
+    given_share = raw / jnp.sum(raw, axis=0, keepdims=True)
+    expert = lax.broadcasted_iota(jnp.int32, (share_tab.shape[1], 1), 0)
+    table = jnp.zeros(share_tab.shape[1:], jnp.float32)
+    for k in range(TOPK):
+        hit = ids_ref[k : k + 1] == expert
+        table = table + jnp.where(hit, given_share[k : k + 1], 0.0)
+    share_tab[me] = table
+    share_copy(me, UPN).start()
+    pl.when(inner == 1)(share_copy(me, DOWNN).start)
+    share_copy(me, ACROSS).start()
+    share_copy(me, TWIN).start()
+    attn_all = attn.at[pl.ds(tokens, tokens)]
+    residual_sent = send(
+        res_ref.at[:, pair_columns], res_pair, near_send.at[1], near_recv.at[1], ACROSS
+    )
+
+    def onward(b, nb, copier):
+        pl.when(nb < inner)(copier(b, UPN).start)
+        pl.when((nb > inner) & (inner == 1))(copier(b, DOWNN).start)
 
     def happen(code, turn):
         nb = lax.rem(code // 2, 4)
         flag = lax.rem(code, 2)
         kind = code // 8
-
-        def own_line(way):
-            pl.when(flag == 0)(copy(me, P0, way).start)
-            pl.when(flag == 1)(copy(me, P1, way).start)
-
-        pl.when(kind == A_UP)(lambda: own_line(UPN))
-        pl.when(kind == A_DOWN)(lambda: own_line(DOWNN))
-
-        @pl.when(kind == A_PASS)
-        def _():
-            pl.when(flag == 0)(copy(me, Q0, ACROSS).start)
-            pl.when(flag == 1)(copy(me, Q1, ACROSS).start)
+        own_b = block_at(nb, y, core)
+        other_b = block_at(nb, 1 - y, core)
+
+        @pl.when(kind == LINE_A)
+        def _():
+            copy(own_b, ACROSS).wait_recv()
+            onward(own_b, nb, copy)
+            copy(own_b, XWAY).start()
+            copy(own_b, TWIN).start()
+            share_copy(own_b, TWIN).wait_recv()
+            onward(own_b, nb, share_copy)
+            share_copy(own_b, ACROSS).start()
+            share_copy(own_b, TWIN).start()
+
+        @pl.when(kind == LINE_B)
+        def _():
+            copy(other_b, ACROSS).wait_recv()
+            onward(other_b, nb, copy)
+            copy(other_b, XWAY).start()
+            copy(other_b, TWIN).start()
+            share_copy(other_b, TWIN).wait_recv()
+            share_copy(other_b, TWIN).start()
+
+        @pl.when((kind == CROSS_A) | (kind == CROSS_B))
+        def _():
+            arrival, forward = taken(jnp.where(kind == CROSS_A, own_b, other_b))
+            arrival.wait_recv()
+            forward.start()
+
+        fresh = block_at(inner, 1 - y, core)
+        pl.when(kind == A_UP)(copy(fresh, UPN).start)
+        pl.when(kind == A_DOWN)(copy(fresh, DOWNN).start)
 
         @pl.when(kind == ATTEND)
         def _():
             @pl.when(turn == 0)
             def _():
-                share_out()
                 for load in loads:
                     load.start()
                 for fetch in fetches:
                     fetch.wait()
 
             attend_step(turn)
+            columns = pl.ds(pl.multiple_of(turn * PACK * HEAD, HEAD), PACK * HEAD)
+            send(
+                attn.at[pl.ds(0, tokens), columns], attn.at[pl.ds(tokens, tokens), columns],
+                near_send.at[0], near_recv.at[0], ACROSS,
+            ).start()
+
+        @pl.when(kind == READY)
+        def _():
+            residual_sent.start()
+            send(attn_all, attn_all, near_send.at[0], near_recv.at[0], ACROSS).wait_recv()
 
         pl.when(kind == PROJECT)(lambda: project(nb, flag == 1))
-        own_b = block_at(nb, y, core)
-        other_b = block_at(nb, 1 - y, core)
-
-        def line(what):
-            pl.when(nb < inner)(copy(own_b, what, UPN).start)
-            pl.when((nb > inner) & (inner == 1))(copy(own_b, what, DOWNN).start)
-
-        @pl.when(kind == P0)
-        def _():
-            arrived(own_b, P0)
-            line(P0)
-            copy(own_b, Q0, ACROSS).start()
-            copy(own_b, PR, XWAY).start()
-            copy(own_b, P0, TWIN).start()
-            share_copy(own_b, TWIN).wait_recv()
-            pl.when(nb < inner)(share_copy(own_b, UPN).start)
-            pl.when((nb > inner) & (inner == 1))(share_copy(own_b, DOWNN).start)
-            share_copy(own_b, ACROSS).start()
-            share_copy(own_b, TWIN).start()
-
-        @pl.when(kind == P1)
-        def _():
-            arrived(own_b, P1)
-            line(P1)
-            copy(own_b, Q1, ACROSS).start()
-            copy(own_b, P1, TWIN).start()
-
-        @pl.when(kind == PR)
-        def _():
-            arrived(own_b, PR)
-            copy(own_b, PR, TWIN).start()
-
-        @pl.when(kind == Q0)
-        def _():
-            arrived(other_b, Q0)
-            copy(other_b, QS, XWAY).start()
-            copy(other_b, Q0, TWIN).start()
-            share_copy(other_b, TWIN).wait_recv()
-            share_copy(other_b, TWIN).start()
-
-        @pl.when(kind == Q1)
-        def _():
-            arrived(other_b, Q1)
-            copy(other_b, Q1, TWIN).start()
-
-        @pl.when(kind == QS)
-        def _():
-            arrived(other_b, QS)
-            copy(other_b, QS, TWIN).start()
 
     length = length_ref[place.me]
     per_group = HEADS // KV_HEADS // PACK
@@ -459,11 +440,11 @@
             nv_ref[:, columns], length, tokens,
         )
         for j in range(PACK):
-            attn[:, pl.ds(pl.multiple_of((i * PACK + j) * HEAD, HEAD), HEAD)] = out[
+            attn[:tokens, pl.ds(pl.multiple_of((i * PACK + j) * HEAD, HEAD), HEAD)] = out[
                 j * tokens : (j + 1) * tokens
             ]
 
-    mixed_ref[...] = res_ref[...].astype(jnp.float32)
+    mixed_ref[...] = jnp.zeros(mixed_ref.shape, jnp.float32)
     chosen = lax.broadcasted_iota(jnp.int32, (1, share_tab.shape[1]), 1) == me
 
     def project(nb, is_own):
@@ -478,7 +459,7 @@
             column = jnp.sum(jnp.where(chosen, turned, 0.0), axis=1, keepdims=True)
             share_col[first + c] = jnp.broadcast_to(column, share_col.shape[1:])
         mine = attn[:, pl.ds(pl.multiple_of(first * depth, 2 * depth), 2 * depth)]
-        weight = held[pl.ds(first, 2)].reshape(2 * depth, D)
+        weight = held[pl.ds(first, 2)].reshape(2 * depth, wide)
         mixed_ref[...] += jnp.dot(mine, weight, preferred_element_type=jnp.float32)
 
     a_words = -(-max(len(A_END), len(A_INNER)) // 4)
@@ -496,24 +477,27 @@
 
     lax.fori_loop(0, a_words, gather_route, jnp.int32(0))
     half_rows = tokens // 2
+    residual_sent.wait_recv()
+    mixed_ref[:tokens] += res_ref[:, my_columns].astype(jnp.float32)
+    mixed_ref[tokens:] += res_pair[...].astype(jnp.float32)
     mixed = mixed_ref[...]
-    scale = lax.rsqrt(jnp.mean(mixed * mixed, axis=-1, keepdims=True) + 1e-06)
-    normed = (mixed * scale * gain_ref[...]).astype(jnp.bfloat16)
+    square = jnp.sum(mixed * mixed, axis=1, keepdims=True)
+    squares[0] = jnp.broadcast_to(square, (2 * tokens, HEAD)).T[: squares.shape[1]]
+    square_sent = send(squares.at[0], squares.at[1], near_send.at[2], near_recv.at[2], ACROSS)
+    square_sent.start()
+    square_sent.wait_recv()
+    theirs = squares[1].T[:, :1]
+    theirs = jnp.concatenate([theirs[tokens:], theirs[:tokens]], axis=0)
+    scale = lax.rsqrt((square + theirs) * (1.0 / D) + 1e-06)
+    normed = (mixed * scale * gain_ref[:, my_columns]).astype(jnp.bfloat16)
 
     def slot(zb, p, yb, c):
         return ((zb * 2 + p) * PAIR + yb) * 2 + c
 
-    sub = half_rows // SUBS
     for p in range(2):
-        for h in range(SUBS):
-            first_row = p * half_rows + h * sub
-            rows[slot(z, p, y, core) * SUBS + h] = normed[first_row : first_row + sub]
-
-    def send(source, dest, send_one, recv_one, way):
-        return pltpu.make_async_remote_copy(
-            src_ref=source, dst_ref=dest, send_sem=send_one, recv_sem=recv_one,
-            device_id=device(way), device_id_type=pl.DeviceIdType.MESH,
-        )
+        base = slot(z, p, y, core) * SUBS
+        rows[base + y] = normed[p * half_rows : (p + 1) * half_rows]
+        rows[base + 1 - y] = normed[tokens + p * half_rows : tokens + (p + 1) * half_rows]
 
     def row_copy(b, h, way):
         t = b * SUBS + h
@@ -549,14 +533,27 @@
         first = slot(zb, p, 0, 0)
         bulk = rows.at[pl.ds(0, 2 * SUBS)]
         send(bulk, bulk, row_send.at[TWIN], twin_rows.at[first // 4], TWIN).wait_recv()
-        x = rows[pl.ds(first * SUBS, 4 * SUBS)].reshape(4 * half_rows, D)
         here = pl.ds(pl.multiple_of(p * half_rows, half_rows), half_rows)
-        share = share_col[pl.ds(place.block(zb, 0, 0), 4), here].reshape(4 * half_rows, HEAD)
-        gate = jnp.dot(x, wg[...], preferred_element_type=jnp.float32)
-        up = jnp.dot(x, wu[...], preferred_element_type=jnp.float32)
+        block = place.block(zb, 0, 0)
+        share = jnp.concatenate(
+            [share_col[block + yb * 2 + c, here] for c in range(2) for yb in range(2)], axis=0
+        )
+        sides = [
+            rows[pl.ds((first + 2 * k) * SUBS, 2 * SUBS)].reshape(4 * half_rows, wide)
+            for k in range(2)
+        ]
+
+        def times(w):
+            return jnp.dot(sides[0], w[:wide], preferred_element_type=jnp.float32) + jnp.dot(
+                sides[1], w[wide:], preferred_element_type=jnp.float32
+            )
+
+        gate, up = times(wg), times(wu)
         act = (gate / (1.0 + jnp.exp(-gate)) * up).astype(jnp.bfloat16)
         out = jnp.dot(act, wd[...], preferred_element_type=jnp.float32) * share[:, :1]
-        part[pl.ds(first, 4)] = out.astype(jnp.bfloat16).reshape(4, half_rows, D)
+        out = out.astype(jnp.bfloat16)
+        for k in range(4):
+            part[first + k % 2 * 2 + k // 2] = out[k * half_rows : (k + 1) * half_rows]
         to_twin(zb, p, 0).start()
         to_twin(zb, p, 1).start()
 
@@ -595,15 +592,15 @@
 
         @pl.when(kind == 2)
         def _():
+            acc[:, my_columns] += mixed_ref[pl.ds(tokens + half_rows, half_rows)]
             part[b] = acc[...].astype(jnp.bfloat16)
             to_pair(z, 1).start()
 
         def close(p, t):
             here = pl.ds(p * half_rows, half_rows)
             to_pair(z, p).wait_recv()
-            out_ref[here] = (
-                acc[...] + mixed_ref[here] + from_pair[t].astype(jnp.float32)
-            ).astype(jnp.bfloat16)
+            acc[:, my_columns] += mixed_ref[here]
+            out_ref[here] = (acc[...] + from_pair[t].astype(jnp.float32)).astype(jnp.bfloat16)
 
         pl.when(kind == 0)(lambda: close(0, z))
         pl.when(kind == 1)(lambda: close(1, LINE))
@@ -647,7 +644,13 @@
 
         @pl.when(kind == PAIR_UP)
         def _():
-            part[slot(zb, 0, 1 - y, core)] = with_twin(zb, 0, 1 - y).astype(jnp.bfloat16)
+            acc[...] = with_twin(zb, 0, 1 - y)
+
+            @pl.when(nb == inner)
+            def _():
+                acc[:, my_columns] += mixed_ref[pl.ds(tokens, half_rows)]
+
+            part[slot(zb, 0, 1 - y, core)] = acc[...].astype(jnp.bfloat16)
             to_pair(zb, 0).start()
 
         pl.when(kind == FOLD)(lambda: fold(nb, piece))
@@ -675,10 +678,10 @@
         pl.when(inner == 0)(at_end)
         pl.when(inner == 1)(at_inner)
 
-    lines = 2 * half
+    lines = pl.ds(0, long)
     sent_by_place(
-        lambda: sent(held.at[0, pl.ds(0, lines)], send_sem.at[UPN]),
-        lambda: sent(held.at[pl.ds(0, 2), pl.ds(0, lines)], send_sem.at[UPN]),
+        lambda: sent(held.at[pl.ds(0, 2), lines], send_sem.at[UPN]),
+        lambda: sent(held.at[pl.ds(0, 4), lines], send_sem.at[UPN]),
     )
     sent_by_place(
         lambda: sent(share_tab.at[pl.ds(0, 1)], share_send.at[UPN]),
@@ -691,12 +694,15 @@
 
     @pl.when(inner == 1)
     def _():
-        sent(held.at[pl.ds(0, 3), pl.ds(0, lines)], send_sem.at[DOWNN])
+        sent(held.at[pl.ds(0, 6), lines], send_sem.at[DOWNN])
         sent(share_tab.at[pl.ds(0, 3)], share_send.at[DOWNN])
         sent(rows.at[pl.ds(0, 9 * SUBS)], row_send.at[DOWNN])
 
-    sent(held.at[pl.ds(0, LINE), pl.ds(0, depth - half)], send_sem.at[ACROSS])
-    sent(held.at[pl.ds(0, LINE - 1), pl.ds(0, lines)], send_sem.at[XWAY])
+    sent(held.at[0, lines], send_sem.at[ACROSS])
+    sent(held.at[pl.ds(0, 2 * LINE - 1), pl.ds(0, short)], send_sem.at[XWAY])
+    sent(attn_all, near_send.at[0])
+    residual_sent.wait_send()
+    square_sent.wait_send()
     sent(held.at[pl.ds(0, 2 * LINE)], send_sem.at[TWIN])
     sent(share_tab.at[pl.ds(0, LINE)], share_send.at[ACROSS])
     sent(share_tab.at[pl.ds(0, 2 * LINE)], share_send.at[TWIN])
@@ -727,12 +733,14 @@
             pltpu.VMEM(queries.shape, jnp.bfloat16),
             pltpu.VMEM(cache_keys.shape, jnp.bfloat16),
             pltpu.VMEM(cache_values.shape, jnp.bfloat16),
-            pltpu.VMEM((devices,) + o_weight.shape, jnp.bfloat16),
-            pltpu.VMEM((tokens, width), jnp.bfloat16),
-            pltpu.VMEM((tokens, D), jnp.float32),
+            pltpu.VMEM((devices, o_weight.shape[0], D // 2), jnp.bfloat16),
+            pltpu.VMEM((2 * tokens, width), jnp.bfloat16),
+            pltpu.VMEM((2 * tokens, D // 2), jnp.float32),
+            pltpu.VMEM((tokens, D // 2), jnp.bfloat16),
+            pltpu.VMEM((2, 8, 2 * tokens), jnp.float32),
             pltpu.VMEM((devices, devices, tokens), jnp.float32),
             pltpu.VMEM((devices, tokens, HEAD), jnp.float32),
-            pltpu.VMEM((2 * devices * SUBS, half // SUBS, D), jnp.bfloat16),
+            pltpu.VMEM((2 * devices * SUBS, half, D // 2), jnp.bfloat16),
             held(2 * devices),
             held(devices),
             held(LINE + 1),
@@ -744,8 +752,10 @@
             dma,
             dma((6,)),
             dma((5,)),
-            dma((devices // 2, 3)),
+            dma((devices // 2, 2)),
             dma((devices // 2,)),
+            dma((3,)),
+            dma((3,)),
             dma((4,)),
             dma((devices,)),
             dma((4,)),

time: 125 us -> 121 us (0.968)
  Pallas kernels: 121 us -> 118 us
    pallas_call x1, Pallas kernels: 121 us -> 118 us  [layer(): pl.pallas_call(layer_kernel, in_specs=[pl.BlockSpec(memory_space=pltpu.SM...]
where the time goes in v5:
time: 121 us; the launch traced here: 120 us
  Pallas kernels  118 us (98%)
  local copies, waits for them, and re-layouts  1.88 us (2%)
    pallas_call x1, Pallas kernels, layer(): pl.pallas_call(layer_kernel, in_specs=[pl.BlockSpec(memory_space=pltpu.SM...  118 us

profile of v5, /device:TPU:0, one launch (start us, length us, event | category | flops | bytes accessed | tf_op | source)
XLA Modules:
  0.0 120.0 jit_solution(8764694339955273285)
XLA Ops:
  0.0 118.1 %shard_map.136 = bf16[128,2048]{1,0:T(8,128)(2,1)} custom-call(s32[16]{0:T(128)} %length_ref.1, bf16[128,256]{1,0:T(8,128)(2,1)} %nk_ref.1, bf16[128,256]{1,0:T(8,128)(2,1)} %nv_ref.1, bf16[128,2048]{1,0:T(8,128)(2,1)} %res_ref.1, f32[1,2048]{1,0:T(1,128)} %bitcast.9, s32[8,128]{1,0:T(8,128)} %bitcast.10, f32[8,128]{1,0:T(8,128)} %bitcast.11, ...), custom_call_target="tpu_custom_call" | custom-call | tf_op jit(solution)/shard_map/pallas_call | solution.py:727
  118.1 1.9 %copy.16 = bf16[128,2048]{1,0:T(8,128)(2,1)} copy(bf16[128,2048]{1,0:T(8,128)(2,1)} %shard_map.136) | data formatting | bytes 1048576

commit v6 on v5

--- a/solution.py
+++ b/solution.py
@@ -262,7 +262,8 @@
     held, attn, mixed_ref, res_pair, squares, share_tab, share_col, rows, part, from_twin,
     from_pair, from_line, acc, wg, wu, wd,
     own_sem, load_sem, send_sem, recv_sem, recv_twin, near_send, near_recv, share_send,
-    share_recv, row_send, row_recv, twin_rows, back_send, twin_sem, pair_sem, line_sem,
+    share_recv, row_send, row_recv, twin_rows, square_send, square_recv,
+    twin_squares, back_send, twin_sem, pair_sem, line_sem,
 ):
     place = Place()
     z, y, core = place.z, place.y, place.core
@@ -482,22 +483,31 @@
     mixed_ref[tokens:] += res_pair[...].astype(jnp.float32)
     mixed = mixed_ref[...]
     square = jnp.sum(mixed * mixed, axis=1, keepdims=True)
-    squares[0] = jnp.broadcast_to(square, (2 * tokens, HEAD)).T[: squares.shape[1]]
-    square_sent = send(squares.at[0], squares.at[1], near_send.at[2], near_recv.at[2], ACROSS)
-    square_sent.start()
-    square_sent.wait_recv()
-    theirs = squares[1].T[:, :1]
-    theirs = jnp.concatenate([theirs[tokens:], theirs[:tokens]], axis=0)
-    scale = lax.rsqrt((square + theirs) * (1.0 / D) + 1e-06)
-    normed = (mixed * scale * gain_ref[:, my_columns]).astype(jnp.bfloat16)
+    gained = (mixed * gain_ref[:, my_columns]).astype(jnp.bfloat16)
 
     def slot(zb, p, yb, c):
         return ((zb * 2 + p) * PAIR + yb) * 2 + c
 
     for p in range(2):
-        base = slot(z, p, y, core) * SUBS
-        rows[base + y] = normed[p * half_rows : (p + 1) * half_rows]
-        rows[base + 1 - y] = normed[tokens + p * half_rows : tokens + (p + 1) * half_rows]
+        mine = slot(z, p, y, core)
+        own_half = slice(p * half_rows, (p + 1) * half_rows)
+        pair_half = slice(tokens + p * half_rows, tokens + (p + 1) * half_rows)
+        rows[mine * SUBS + y] = gained[own_half]
+        rows[mine * SUBS + 1 - y] = gained[pair_half]
+        both = jnp.where(
+            y == 0,
+            jnp.concatenate([square[own_half], square[pair_half]], axis=0),
+            jnp.concatenate([square[pair_half], square[own_half]], axis=0),
+        )
+        squares[mine] = jnp.broadcast_to(both, (tokens, HEAD)).T[: squares.shape[1]]
+
+    def square_copy(b, way):
+        landed = twin_squares.at[b // 4] if way == TWIN else square_recv.at[b // 2]
+        return send(squares.at[b], squares.at[b], square_send.at[way], landed, way)
+
+    def pass_on(b, h, way):
+        row_copy(b, h, way).start()
+        pl.when(h == 0)(square_copy(b, way).start)
 
     def row_copy(b, h, way):
         t = b * SUBS + h
@@ -533,6 +543,11 @@
         first = slot(zb, p, 0, 0)
         bulk = rows.at[pl.ds(0, 2 * SUBS)]
         send(bulk, bulk, row_send.at[TWIN], twin_rows.at[first // 4], TWIN).wait_recv()
+        few = squares.at[pl.ds(0, 2)]
+        send(few, few, square_send.at[TWIN], twin_squares.at[first // 4], TWIN).wait_recv()
+        totals = [squares[first + c] + squares[first + 2 + c] for c in range(2)]
+        total = jnp.concatenate(totals, axis=1)
+        scale = lax.rsqrt(total * (1.0 / D) + 1e-06).T[:, :1]
         here = pl.ds(pl.multiple_of(p * half_rows, half_rows), half_rows)
         block = place.block(zb, 0, 0)
         share = jnp.concatenate(
@@ -544,9 +559,9 @@
         ]
 
         def times(w):
-            return jnp.dot(sides[0], w[:wide], preferred_element_type=jnp.float32) + jnp.dot(
-                sides[1], w[wide:], preferred_element_type=jnp.float32
-            )
+            first_half = jnp.dot(sides[0], w[:wide], preferred_element_type=jnp.float32)
+            other_half = jnp.dot(sides[1], w[wide:], preferred_element_type=jnp.float32)
+            return (first_half + other_half) * scale
 
         gate, up = times(wg), times(wu)
         act = (gate / (1.0 + jnp.exp(-gate)) * up).astype(jnp.bfloat16)
@@ -619,19 +634,20 @@
         def _():
             b = slot(zb, p, yb, core)
             row_copy(b, h, ACROSS).wait_recv()
+            pl.when(h == 0)(square_copy(b, ACROSS).wait_recv)
             onward = piece != PD
-            pl.when(onward & (nb < inner))(row_copy(b, h, UPN).start)
-            pl.when(onward & (nb > inner) & (inner == 1))(row_copy(b, h, DOWNN).start)
-            pl.when((piece == PC) & (nb != inner))(row_copy(b, h, ACROSS).start)
-            row_copy(b, h, TWIN).start()
-
-        pl.when(kind == UP_OWN)(row_copy(own_piece, h, UPN).start)
-        pl.when(kind == DOWN_OWN)(row_copy(own_piece, h, DOWNN).start)
+            pl.when(onward & (nb < inner))(lambda: pass_on(b, h, UPN))
+            pl.when(onward & (nb > inner) & (inner == 1))(lambda: pass_on(b, h, DOWNN))
+            pl.when((piece == PC) & (nb != inner))(lambda: pass_on(b, h, ACROSS))
+            pass_on(b, h, TWIN)
+
+        pl.when(kind == UP_OWN)(lambda: pass_on(own_piece, h, UPN))
+        pl.when(kind == DOWN_OWN)(lambda: pass_on(own_piece, h, DOWNN))
 
         @pl.when(kind == PASS_OWN)
         def _():
-            row_copy(own_piece, h, ACROSS).start()
-            row_copy(own_piece, h, TWIN).start()
+            pass_on(own_piece, h, ACROSS)
+            pass_on(own_piece, h, TWIN)
 
         @pl.when(kind == SERVE)
         def _():
@@ -690,6 +706,10 @@
     sent_by_place(
         lambda: sent(rows.at[pl.ds(0, 3 * SUBS)], row_send.at[UPN]),
         lambda: sent(rows.at[pl.ds(0, 6 * SUBS)], row_send.at[UPN]),
+    )
+    sent_by_place(
+        lambda: sent(squares.at[pl.ds(0, 3)], square_send.at[UPN]),
+        lambda: sent(squares.at[pl.ds(0, 6)], square_send.at[UPN]),
     )
 
     @pl.when(inner == 1)
@@ -697,17 +717,19 @@
         sent(held.at[pl.ds(0, 6), lines], send_sem.at[DOWNN])
         sent(share_tab.at[pl.ds(0, 3)], share_send.at[DOWNN])
         sent(rows.at[pl.ds(0, 9 * SUBS)], row_send.at[DOWNN])
+        sent(squares.at[pl.ds(0, 9)], square_send.at[DOWNN])
 
     sent(held.at[0, lines], send_sem.at[ACROSS])
     sent(held.at[pl.ds(0, 2 * LINE - 1), pl.ds(0, short)], send_sem.at[XWAY])
     sent(attn_all, near_send.at[0])
     residual_sent.wait_send()
-    square_sent.wait_send()
     sent(held.at[pl.ds(0, 2 * LINE)], send_sem.at[TWIN])
     sent(share_tab.at[pl.ds(0, LINE)], share_send.at[ACROSS])
     sent(share_tab.at[pl.ds(0, 2 * LINE)], share_send.at[TWIN])
     sent(rows.at[pl.ds(0, 5 * SUBS)], row_send.at[ACROSS])
     sent(rows.at[pl.ds(0, 4 * LINE * SUBS)], row_send.at[TWIN])
+    sent(squares.at[pl.ds(0, 5)], square_send.at[ACROSS])
+    sent(squares.at[pl.ds(0, 4 * LINE)], square_send.at[TWIN])
     sent(part.at[pl.ds(0, 7 * LINE + 2)], back_send.at[0])
 
 
@@ -737,7 +759,7 @@
             pltpu.VMEM((2 * tokens, width), jnp.bfloat16),
             pltpu.VMEM((2 * tokens, D // 2), jnp.float32),
             pltpu.VMEM((tokens, D // 2), jnp.bfloat16),
-            pltpu.VMEM((2, 8, 2 * tokens), jnp.float32),
+            pltpu.VMEM((2 * devices, 8, tokens), jnp.float32),
             pltpu.VMEM((devices, devices, tokens), jnp.float32),
             pltpu.VMEM((devices, tokens, HEAD), jnp.float32),
             pltpu.VMEM((2 * devices * SUBS, half, D // 2), jnp.bfloat16),
@@ -754,12 +776,15 @@
             dma((5,)),
             dma((devices // 2, 2)),
             dma((devices // 2,)),
-            dma((3,)),
-            dma((3,)),
+            dma((2,)),
+            dma((2,)),
             dma((4,)),
             dma((devices,)),
             dma((4,)),
             dma((devices * SUBS,)),
+            dma((devices // 2,)),
+            dma((4,)),
+            dma((devices,)),
             dma((devices // 2,)),
             dma((1,)),
             dma((devices,)),

time: 121 us -> 119 us (0.983)
    pallas_call x1, Pallas kernels: 118 us -> 117 us  [layer(): pl.pallas_call(layer_kernel, in_specs=[pl.BlockSpec(memory_space=pltpu.SM...]
where the time goes in v6:
time: 119 us
  Pallas kernels  117 us (98%)
  local copies, waits for them, and re-layouts  1.88 us (2%)
    pallas_call x1, Pallas kernels, layer(): pl.pallas_call(layer_kernel, in_specs=[pl.BlockSpec(memory_space=pltpu.SM...  117 us

profile of v6, /device:TPU:0, one launch (start us, length us, event | category | flops | bytes accessed | tf_op | source)
XLA Modules:
  0.0 118.8 jit_solution(4589955026004263341)
XLA Ops:
  0.0 116.9 %shard_map.136 = bf16[128,2048]{1,0:T(8,128)(2,1)} custom-call(s32[16]{0:T(128)} %length_ref.1, bf16[128,256]{1,0:T(8,128)(2,1)} %nk_ref.1, bf16[128,256]{1,0:T(8,128)(2,1)} %nv_ref.1, bf16[128,2048]{1,0:T(8,128)(2,1)} %res_ref.1, f32[1,2048]{1,0:T(1,128)} %bitcast.9, s32[8,128]{1,0:T(8,128)} %bitcast.10, f32[8,128]{1,0:T(8,128)} %bitcast.11, ...), custom_call_target="tpu_custom_call" | custom-call | tf_op jit(solution)/shard_map/pallas_call | solution.py:749
  116.9 1.9 %copy.16 = bf16[128,2048]{1,0:T(8,128)(2,1)} copy(bf16[128,2048]{1,0:T(8,128)(2,1)} %shard_map.136) | data formatting | bytes 1048576

commit v7 on v6

--- a/solution.py
+++ b/solution.py
@@ -179,14 +179,14 @@
 A_KINDS = {"A": LINE_A, "B": LINE_B, "XA": CROSS_A, "XB": CROSS_B}
 A_PLAIN = {"u": A_UP, "d": A_DOWN, "a": ATTEND, "r": READY}
 A_END = (
-    "a", "a", "a", "0B", "u", "a", "a", "a", "1A", "1B", "a", "2A",
-    "a", "3A", "1XA", "2XA", "1XB", "0XB", "r", "2B", "j10", "j21", "j01", "3XA",
-    "2XB", "3B", "j00", "j20", "j11", "3XB", "j31", "j30",
+    "a", "a", "a", "a", "0B", "u", "1A", "a", "a", "a", "a", "2A",
+    "3A", "0XB", "r", "2XA", "1XA", "1B", "j00", "2B", "j01", "3XA", "j21", "1XB",
+    "j11", "3B", "2XB", "j31", "j10", "j20", "3XB", "j30",
 )
 A_INNER = (
-    "a", "a", "2A", "0A", "1B", "u", "d", "a", "a", "3A", "0B", "a",
-    "a", "2B", "a", "3B", "a", "1XB", "0XB", "2XA", "3XA", "2XB", "0XA", "3XB",
-    "r", "j11", "j21", "j20", "j30", "j01", "j31", "j10", "j00",
+    "a", "a", "2A", "0A", "1B", "d", "a", "a", "u", "3A", "a", "0B",
+    "a", "2B", "a", "a", "2XA", "3B", "0XA", "0XB", "2XB", "3XA", "r", "j11",
+    "1XB", "j20", "j01", "3XB", "j21", "j10", "j31", "j00", "j30",
 )
 
 

time: 119 us -> 118 us (level)
    pallas_call x1, Pallas kernels: 117 us -> 116 us  [layer(): pl.pallas_call(layer_kernel, in_specs=[pl.BlockSpec(memory_space=pltpu.SM...]
where the time goes in v7:
time: 118 us; the launch traced here: 117 us
  Pallas kernels  116 us (98%)
  local copies, waits for them, and re-layouts  1.88 us (2%)
    pallas_call x1, Pallas kernels, layer(): pl.pallas_call(layer_kernel, in_specs=[pl.BlockSpec(memory_space=pltpu.SM...  116 us

profile of v7, /device:TPU:0, one launch (start us, length us, event | category | flops | bytes accessed | tf_op | source)
XLA Modules:
  0.0 117.5 jit_solution(3887055376935747083)
XLA Ops:
  0.0 115.6 %shard_map.136 = bf16[128,2048]{1,0:T(8,128)(2,1)} custom-call(s32[16]{0:T(128)} %length_ref.1, bf16[128,256]{1,0:T(8,128)(2,1)} %nk_ref.1, bf16[128,256]{1,0:T(8,128)(2,1)} %nv_ref.1, bf16[128,2048]{1,0:T(8,128)(2,1)} %res_ref.1, f32[1,2048]{1,0:T(1,128)} %bitcast.9, s32[8,128]{1,0:T(8,128)} %bitcast.10, f32[8,128]{1,0:T(8,128)} %bitcast.11, ...), custom_call_target="tpu_custom_call" | custom-call | tf_op jit(solution)/shard_map/pallas_call | solution.py:749
  115.6 1.9 %copy.16 = bf16[128,2048]{1,0:T(8,128)(2,1)} copy(bf16[128,2048]{1,0:T(8,128)(2,1)} %shard_map.136) | data formatting | bytes 1048576
